TPU v7x, 128 devices: a whole 4x4x4 slice. The times are simulated.
128 devices in a mesh: dp: 64 (over x, z, y), rep: 2 (over core).
Axes of the slice: x: 4, y: 4, z: 4, core: 2. Of those that a mesh axis runs over, the one named last changes fastest.
Arguments:
- pooled: bfloat16 [16, 128, 32768], P(None, ('dp', 'rep')), may hold values from -6 to 6
- slot_of_block: int32 [128], replicated, may hold values from 0 to 127, each once
- dense_part: bfloat16 [128, 32768], P(None, ('dp', 'rep')), may hold values from -6 to 6
- labels: int32 [32768], P(('dp', 'rep')), may hold values 0 or 1
- sample_weight: float32 [32768], P(('dp', 'rep')), may hold values from 0.5 to 18, as said below
- proj_wide: bfloat16 [6, 256, 128], replicated, may hold values from -0.375 to 0.375
- proj_mid: bfloat16 [4, 64, 128], replicated, may hold values from -0.75 to 0.75
- proj_narrow: bfloat16 [16, 16, 128], replicated, may hold values from -1.5 to 1.5
- cross_in: bfloat16 [2, 3456, 256], replicated, may hold values from -0.109375 to 0.109375
- cross_out: bfloat16 [2, 256, 3456], replicated, may hold values from -0.375 to 0.375
- cross_bias: float32 [2, 3456], replicated, may hold values from -3 to 3
- head_weight: float32 [3456], replicated, may hold values from -0.24 to 0.24
Outputs:
- pooled_grad: float32 [16, 128, 32768], P(None, ('dp', 'rep'))
- grad_cross_in: float32 [2, 3456, 256], P(None, ('dp', 'rep'))
- grad_cross_out: float32 [2, 256, 3456], P(None, None, ('dp', 'rep'))
- grad_bias: float32 [2, 3456], P(None, ('dp', 'rep'))
Inputs may be any that keep to these rules, and one draw needn't show every extreme that they name: `slot_of_block`: each number of 0 to 127 appears once. `sample_weight`: positive.
All inputs are finite; a program needn't handle non-finite values. No bound on the sum of `labels` on one device may be relied on, other than what follows from the above.
Results may differ from a plain program's by a relative error of at most 0.014.
Values may be sent and summed in bfloat16 or wider, within the bound.
A program may use at most 128 MiB of HBM per device.

v0:
```python
import jax
import jax.numpy as jnp
from jax import lax
from jax.sharding import Mesh
from jax.sharding import PartitionSpec as P

BLOCK_WIDTH = 16
WIDE_TABLES = 6
MID_TABLES = 4
NARROW_TABLES = 16
WIDE_WIDTH = 256
MID_WIDTH = 64
NARROW_WIDTH = 16
PROJECTED = 128
LAYERS = 2
BLOCKS = 128
DP = ("dp_0", "dp_1", "dp_2")
DP_REP = ("dp_0", "dp_1", "dp_2", "rep")


def split_up(shard, dim, devices):
    before, after = (shard.shape[:dim], shard.shape[dim + 1 :])
    return jnp.moveaxis(shard.reshape(*before, devices, -1, *after), dim, 0)


def joined_along(tiles, dim):
    dims = list(tiles.shape[1:])
    dims[dim] *= tiles.shape[0]
    return jnp.moveaxis(tiles, 0, dim).reshape(dims)


def one_exchange(shard, axis, axes, splits, concats):
    sizes = [lax.axis_size(a) for a in axes]
    tiles = split_up(shard, splits[0], sizes[0])
    tiles = jnp.moveaxis(split_up(tiles, splits[1] + 1, sizes[1]), 0, 1)
    inside = tiles.shape[2:]
    tiles = tiles.reshape(-1, *inside)
    tiles = lax.all_to_all(tiles, axis, split_axis=0, concat_axis=0, tiled=True)
    tiles = joined_along(tiles.reshape(*sizes, *inside), concats[0] + 1)
    return joined_along(tiles, concats[1])


def one_axis_at_a_time(shard, axes):
    for axis in axes:
        shard = lax.psum(shard, axis)
    return shard


def own_tiles(shard, axis, dim):
    devices = lax.axis_size(axis)
    tiles = split_up(shard, dim, devices)
    lines = tiles.reshape(devices, -1)
    extent = max(16, -(-lines.shape[1] // 1024) * 8)
    lines = jnp.pad(lines, ((0, 0), (0, extent * 128 - lines.shape[1]))).reshape(-1, 128)
    own = lax.psum_scatter(lines, axis, scatter_dimension=0, tiled=True)
    return own.reshape(-1)[: tiles[0].size].reshape(tiles.shape[1:])


def table_layout():
    first_end = WIDE_TABLES * (WIDE_WIDTH // BLOCK_WIDTH)
    second_end = first_end + MID_TABLES * (MID_WIDTH // BLOCK_WIDTH)
    return (
        (0, first_end, WIDE_TABLES, WIDE_WIDTH),
        (first_end, second_end, MID_TABLES, MID_WIDTH),
        (second_end, BLOCKS, NARROW_TABLES, NARROW_WIDTH),
    )


def project_tables(logical, proj_tables):
    row_count = logical.shape[2]
    outputs = []
    for layout, proj_table in zip(table_layout(), proj_tables):
        block_start, block_end, table_count, table_width = layout
        pieces = logical[:, block_start:block_end].reshape(
            BLOCK_WIDTH, table_count, table_width // BLOCK_WIDTH, row_count
        )
        matrix = proj_table.reshape(table_count, table_width // BLOCK_WIDTH, BLOCK_WIDTH, PROJECTED)
        result = jnp.einsum("tkco,ctkr->tor", matrix, pieces, preferred_element_type=jnp.float32)
        outputs.append(result.reshape(table_count * PROJECTED, row_count))
    return jnp.concatenate(outputs, 0)


def project_back(proj_grad, proj_tables):
    row_count = proj_grad.shape[1]
    outputs = []
    offset = 0
    for layout, proj_table in zip(table_layout(), proj_tables):
        block_start, block_end, table_count, table_width = layout
        piece = proj_grad[offset : offset + table_count * PROJECTED].reshape(
            table_count, PROJECTED, row_count
        )
        offset = offset + table_count * PROJECTED
        matrix = proj_table.reshape(table_count, table_width // BLOCK_WIDTH, BLOCK_WIDTH, PROJECTED)
        result = jnp.einsum("tkco,tor->ctkr", matrix, piece, preferred_element_type=jnp.float32)
        outputs.append(result.reshape(BLOCK_WIDTH, block_end - block_start, row_count))
    return jnp.concatenate(outputs, 1)


def block_step(
    slots,
    dense_part,
    labels,
    sample_weight,
    slot_of_block,
    proj_tables,
    cross_in,
    cross_out,
    cross_bias,
    head_weight,
):
    logical = jnp.take(slots, slot_of_block, axis=1)
    projected = project_tables(logical, proj_tables)
    start = jnp.concatenate([dense_part.astype(jnp.float32), projected], 0).astype(jnp.bfloat16)
    start_full = start.astype(jnp.float32)
    layer_inputs = [start]
    hidden_list = []
    gate_list = []
    current = start
    for layer in range(LAYERS):
        hidden = jnp.einsum(
            "wk,wr->kr", cross_in[layer], current, preferred_element_type=jnp.float32
        ).astype(jnp.bfloat16)
        gate = (
            jnp.einsum("kw,kr->wr", cross_out[layer], hidden, preferred_element_type=jnp.float32)
            + cross_bias[layer][:, None]
        )
        current = (start_full * gate + current.astype(jnp.float32)).astype(jnp.bfloat16)
        hidden_list.append(hidden)
        gate_list.append(gate)
        layer_inputs.append(current)
    logit = jnp.dot(head_weight, current.astype(jnp.float32), precision=lax.Precision.HIGHEST)
    signal = sample_weight * (jax.nn.sigmoid(logit) - labels.astype(jnp.float32))
    upstream = head_weight[:, None] * signal[None, :]
    start_grad = jnp.zeros(start_full.shape, jnp.float32)
    in_terms = [None] * LAYERS
    out_terms = [None] * LAYERS
    bias_terms = [None] * LAYERS
    for layer in reversed(range(LAYERS)):
        gate_grad = start_full * upstream
        bias_terms[layer] = jnp.sum(gate_grad, axis=1)
        gate_low = gate_grad.astype(jnp.bfloat16)
        out_terms[layer] = jnp.einsum(
            "wr,kr->wk", gate_low, hidden_list[layer], preferred_element_type=jnp.float32
        )
        hidden_grad = jnp.einsum(
            "kw,wr->kr", cross_out[layer], gate_low, preferred_element_type=jnp.float32
        ).astype(jnp.bfloat16)
        in_terms[layer] = jnp.einsum(
            "wr,kr->wk", layer_inputs[layer], hidden_grad, preferred_element_type=jnp.float32
        )
        start_grad = start_grad + gate_list[layer] * upstream
        upstream = upstream + jnp.einsum(
            "wk,kr->wr", cross_in[layer], hidden_grad, preferred_element_type=jnp.float32
        )
    start_grad = start_grad + upstream
    proj_grad = start_grad[PROJECTED:].astype(jnp.bfloat16)
    logical_grad = project_back(proj_grad, proj_tables)
    slot_grad = jnp.zeros(logical_grad.shape, jnp.float32).at[:, slot_of_block, :].set(logical_grad)
    return (slot_grad, jnp.stack(in_terms), jnp.stack(out_terms), jnp.stack(bias_terms))


def body(
    pooled,
    slot_of_block,
    dense_part,
    labels,
    sample_weight,
    proj_wide,
    proj_mid,
    proj_narrow,
    cross_in,
    cross_out,
    cross_bias,
    head_weight,
):
    dp_count = lax.axis_size(DP)
    rep_count = lax.axis_size("rep")
    devices = dp_count * rep_count
    row_count = labels.shape[0]
    blocks_here = pooled.shape[1]
    batch_rows = row_count * devices
    layer_count = cross_in.shape[0]
    received = one_exchange(pooled[:, None, None], DP_REP, (DP, "rep"), (4, 4), (1, 2))
    slots = received.reshape(BLOCK_WIDTH, BLOCKS, row_count)
    local_total = jnp.sum(sample_weight)
    total = one_axis_at_a_time(local_total, DP_REP)
    proj_tables = (proj_wide, proj_mid, proj_narrow)
    slot_grad, in_term, out_term, bias_term = block_step(
        slots,
        dense_part,
        labels,
        sample_weight,
        slot_of_block,
        proj_tables,
        cross_in,
        cross_out,
        cross_bias,
        head_weight,
    )
    sectioned_grad = slot_grad.reshape(
        BLOCK_WIDTH, dp_count, rep_count, blocks_here, 1, 1, row_count
    )
    returned = lax.all_to_all(
        lax.all_to_all(
            sectioned_grad.astype(jnp.bfloat16), DP, split_axis=1, concat_axis=4, tiled=True
        ),
        "rep",
        split_axis=2,
        concat_axis=5,
        tiled=True,
    ).astype(sectioned_grad.dtype)
    returned = returned.reshape(BLOCK_WIDTH, blocks_here, batch_rows)
    weight_terms = jnp.concatenate([in_term, out_term], 0)
    weight_sums = own_tiles(weight_terms.astype(jnp.bfloat16), DP_REP, 1).astype(jnp.float32)
    bias_sums = lax.psum_scatter(bias_term, DP_REP, scatter_dimension=1, tiled=True)
    scale = batch_rows / total
    grad_in = weight_sums[:layer_count] * scale
    grad_out = jnp.swapaxes(weight_sums[layer_count:], 1, 2) * scale
    grad_bias = bias_sums * scale
    return (returned * scale, grad_in, grad_out, grad_bias)


def solution(mesh):
    finer = Mesh(mesh.devices.reshape(4, 4, 4, mesh.shape["rep"]), ("dp_0", "dp_1", "dp_2", "rep"))
    return jax.shard_map(
        body,
        mesh=finer,
        in_specs=(
            P(None, DP_REP, None),
            P(),
            P(None, DP_REP),
            P(DP_REP),
            P(DP_REP),
            P(),
            P(),
            P(),
            P(),
            P(),
            P(),
            P(),
        ),
        out_specs=(
            P(None, DP_REP, None),
            P(None, DP_REP, None),
            P(None, None, DP_REP),
            P(None, DP_REP),
        ),
        check_vma=False,
    )
```

profile of v0, /device:TPU:0, one launch (start us, length us, event | category | flops | bytes accessed | tf_op | source)
XLA Modules:
  0.0 294.4 jit_solution(1450464642006116457)
XLA Ops:
  7.2 1.6 copy.94
  9.1 1.6 copy.69
  10.6 11.2 %all-to-all-start = ((bf16[128,16,1,1,1,256]{5,1,4,3,2,0:T(8,128)(2,1)}), bf16[128,16,1,1,1,256]{5,1,4,3,2,0:T(8,128)(2,1)S(1)}, u32[]{:S(2)}, u32[]{:S(2)}) async-start(bf16[128,16,1,1,1,256]{5,1,4,3,2,0:T(8,128)(2,1)} %bitcast.2), calls=%async_computation | async-start | bytes 2097152 | tf_op jit(solution)/shard_map/all_to_all | solution.py:38
  21.9 0.7 copy.73
  22.6 0.6 reshape.183
  23.2 0.7 slice_reduce_fusion
  23.9 17.0 %all-to-all-done = bf16[128,16,1,1,1,256]{5,1,4,3,2,0:T(8,128)(2,1)S(1)} async-done(((bf16[128,16,1,1,1,256]{5,1,4,3,2,0:T(8,128)(2,1)}), bf16[128,16,1,1,1,256]{5,1,4,3,2,0:T(8,128)(2,1)S(1)}, u32[]{:S(2)}, u32[]{:S(2)}) %all-to-all-start) | async-done | bytes 1048608 | tf_op jit(solution)/shard_map/all_to_all | solution.py:38
  40.9 0.6 gather_fusion
  42.4 0.8 copy.76
  44.5 2.3 fusion.37
  47.2 2.5 fusion.8
  49.9 0.6 fusion.43
  50.6 0.7 fusion.1
  51.4 1.7 fusion.13
  53.8 0.7 fusion.46
  54.5 2.1 convolution_convert_fusion
  56.6 1.8 fusion.11
  58.4 0.8 fusion.40
  59.2 1.0 copy-done.3
  60.2 2.0 convolution_convert_fusion.1
  62.2 0.7 convolution_convert_fusion.2
  62.9 3.8 %concatenate.29 = bf16[1,128,27,256]{3,2,1,0:T(8,128)(2,1)} reshape(bf16[3456,256]{1,0:T(8,128)(2,1)} %convolution_convert_fusion) | data formatting | bytes 3538944 | tf_op jit(solution)/shard_map/concatenate | solution.py:213
  66.7 3.8 %concatenate.28 = bf16[1,128,27,256]{3,2,1,0:T(8,128)(2,1)} reshape(bf16[3456,256]{1,0:T(8,128)(2,1)} %convolution_convert_fusion.1) | data formatting | bytes 3538944 | tf_op jit(solution)/shard_map/concatenate | solution.py:213
  70.5 1.6 concatenate.27
  72.1 3.0 %convolution_convert_fusion.3 = bf16[3456,256]{1,0:T(8,128)(2,1)} fusion(bf16[256,256]{1,0:T(8,128)(2,1)S(1)} %fusion.40, bf16[2048,256]{0,1:T(8,128)(2,1)S(1)} %copy.76, bf16[512,256]{0,1:T(8,128)(2,1)} %copy-done.8, bf16[768,256]{0,1:T(8,128)(2,1)} %copy-done.6, bf16[128,256]{0,1:T(8,128)(2,1)S(1)} %copy-done.12), kind=kOutput, calls=%fused_computation.22 | convolution fusion | flops 460947456 | bytes 3670016 | tf_op jit(solution)/shard_map/wr,kr->wk/dot_general | solution.py:148
  75.1 3.9 %concatenate.26 = bf16[1,128,27,256]{3,2,1,0:T(8,128)(2,1)} reshape(bf16[3456,256]{1,0:T(8,128)(2,1)} %convolution_convert_fusion.3) | data formatting | bytes 3538944 | tf_op jit(solution)/shard_map/concatenate | solution.py:213
  79.0 6.7 %maximum_bitcast_fusion = bf16[128,4,27,256]{3,2,0,1:T(8,128)(2,1)} fusion(bf16[1,128,27,256]{3,2,1,0:T(8,128)(2,1)S(1)} %copy-done.2, bf16[1,128,27,256]{3,2,1,0:T(8,128)(2,1)} %concatenate.28, bf16[1,128,27,256]{3,2,1,0:T(8,128)(2,1)} %concatenate.27, bf16[1,128,27,256]{3,2,1,0:T(8,128)(2,1)} %concatenate.26), kind=kLoop, calls=%fused_computation.2 | loop fusion | flops 10616832 | bytes 14155776 | tf_op jit(solution)/shard_map/transpose | solution.py:23
  85.7 8.0 %copy.83 = bf16[128,4,27,256]{3,2,1,0:T(8,128)(2,1)} copy(bf16[128,4,27,256]{3,2,0,1:T(8,128)(2,1)} %maximum_bitcast_fusion) | data formatting | bytes 14155776 | tf_op jit(solution)/shard_map/transpose | solution.py:23
  93.8 12.5 %reshape.162 = bf16[27648,128]{1,0:T(8,128)(2,1)} reshape(bf16[128,4,27,256]{3,2,1,0:T(8,128)(2,1)} %copy.83) | data formatting | bytes 14155776 | tf_op jit(solution)/shard_map/reshape | solution.py:54
  106.3 0.7 copy-done.21
  107.0 5.7 %fusion.4 = bf16[3456,256]{0,1:T(8,128)(2,1)S(1)} fusion(f32[3456,256]{0,1:T(8,128)} %copy-done.3, bf16[256,256]{1,0:T(8,128)(2,1)S(1)} %fusion.40, f32[3456,256]{0,1:T(8,128)} %copy-done.1, f32[3456,256]{0,1:T(8,128)} %get-tuple-element.31, f32[256]{0:T(256)S(1)} %copy-done.21, f32[3456]{0:T(1024)S(1)} %copy-done.14, bf16[2,3456,256]{2,1,0:T(8,128)(2,1)} %param.20), kind=kOutput, calls=%fused_computation.18 | convolution fusion | flops 459177984 | bytes 14301696 | tf_op jit(solution)/shard_map/wk,kr->wr/dot_general | solution.py:152
  114.5 1.5 maximum_bitcast_fusion.1
  116.2 11.9 %scatter_fusion = f32[16,128,256]{2,0,1:T(8,128)S(1)} fusion(f32[16,128,256]{2,0,1:T(8,128)S(1)} %broadcast_in_dim.18, s32[128]{0:T(128)S(1)} %copy-done.23, f32[128,16,256]{2,1,0:T(8,128)} %maximum_bitcast_fusion.1), kind=kCustom, calls=%fused_computation.1 | custom fusion | bytes 6291968 | tf_op jit(solution)/shard_map/scatter | solution.py:158
  128.1 1.1 convert_element_type.89
  129.2 4.9 %all-to-all-start.1 = ((bf16[16,64,2,1,1,1,256]{6,0,2,5,4,3,1:T(8,128)(2,1)}), bf16[16,64,2,1,1,1,256]{6,0,2,5,4,3,1:T(8,128)(2,1)S(1)}, u32[]{:S(2)}, u32[]{:S(2)}) async-start(bf16[16,64,2,1,1,1,256]{6,0,2,5,4,3,1:T(8,128)(2,1)} %bitcast.47), calls=%async_computation.1 | async-start | bytes 2097152 | tf_op jit(solution)/shard_map/all_to_all | solution.py:204
  134.1 16.6 %psum.28 = f32[]{:T(128)} all-reduce(f32[]{:T(128)} %get-tuple-element.28), channel_id=1, replica_groups=mesh['dp_0'=4,'dp_1'=4,'dp_2'=4,'rep'=2] {'dp_0'}, use_global_device_ids=true, to_apply=%region_2.0 | all-reduce | flops 1 | bytes 8 | tf_op jit(solution)/shard_map/psum | solution.py:45
  150.7 11.1 %psum.29 = f32[]{:T(128)} all-reduce(f32[]{:T(128)} %psum.28), channel_id=1, replica_groups=mesh['dp_0'=4,'dp_1'=4,'dp_2'=4,'rep'=2] {'dp_1'}, use_global_device_ids=true, to_apply=%region_3.0 | all-reduce | flops 1 | bytes 8 | tf_op jit(solution)/shard_map/psum | solution.py:45
  161.8 11.0 %psum.30 = f32[]{:T(128)} all-reduce(f32[]{:T(128)} %psum.29), channel_id=1, replica_groups=mesh['dp_0'=4,'dp_1'=4,'dp_2'=4,'rep'=2] {'dp_2'}, use_global_device_ids=true, to_apply=%region_4.0 | all-reduce | flops 1 | bytes 8 | tf_op jit(solution)/shard_map/psum | solution.py:45
  172.9 3.1 %psum.31 = f32[]{:T(128)} all-reduce(f32[]{:T(128)} %psum.30), channel_id=1, replica_groups=mesh['dp_0'=4,'dp_1'=4,'dp_2'=4,'rep'=2] {'rep'}, use_global_device_ids=true, to_apply=%region_5.6 | all-reduce | flops 1 | bytes 8 | tf_op jit(solution)/shard_map/psum | solution.py:45
  176.7 64.0 %all-reduce.1 = f32[2,3456]{1,0:T(2,128)S(1)} all-reduce(f32[2,3456]{1,0:T(2,128)S(1)} %pad_maximum_fusion.2), channel_id=3, replica_groups=mesh['dp_0'=4,'dp_1'=4,'dp_2'=4,'rep'=2] {'dp_0','dp_1','dp_2','rep'}, use_global_device_ids=true, to_apply=%region_9.10.clone | all-reduce | flops 6912 | bytes 55296
  240.7 0.6 dynamic-slice_multiply_fusion
  241.5 4.6 %all_to_all.32 = bf16[16,1,2,1,64,1,256]{6,0,4,5,3,1,2:T(8,128)(2,1)S(1)} all-to-all(bf16[16,1,2,1,64,1,256]{6,0,4,5,3,1,2:T(8,128)(2,1)S(1)} %copy.81), channel_id=1, replica_groups=mesh['dp_0'=4,'dp_1'=4,'dp_2'=4,'rep'=2] {'rep'}, dimensions={2} | all-to-all | bytes 2097152 | tf_op jit(solution)/shard_map/all_to_all | solution.py:203
  246.3 1.6 copy.82
  248.0 4.1 %mul.105 = f32[16,1,32768]{2,1,0:T(1,128)} reshape(f32[16,1,1,1,64,2,1,256]{7,5,4,0,6,3,2,1:T(2,128)S(1)} %copy.82) | data formatting | bytes 4194304 | tf_op jit(solution)/shard_map/mul | solution.py:220
  252.1 33.3 %reduce-scatter.5.cloned.1.call-done = bf16[216,128]{1,0:T(8,128)(2,1)} async-done(((bf16[27648,128]{1,0:T(8,128)(2,1)}), bf16[216,128]{1,0:T(8,128)(2,1)}) %reduce-scatter.5.cloned.1.call-update) | async-done | bytes 55312
  285.4 0.8 convert_element_type.92
  286.2 0.7 copy.85
  286.9 0.7 copy.86
  (88 shorter events, 6.3 us)
Async XLA Ops:
  7.2 36.8 %copy-start = (bf16[6,256,128]{2,1,0:T(8,128)(2,1)S(1)}, bf16[6,256,128]{2,1,0:T(8,128)(2,1)}, u32[]{:S(2)}) copy-start(bf16[6,256,128]{2,1,0:T(8,128)(2,1)} %param.17) | copy-start | bytes 1179652
  8.9 13.0 %copy-start.10 = (bf16[128,256]{1,0:T(8,128)(2,1)S(1)}, bf16[128,256]{1,0:T(8,128)(2,1)}, u32[]{:S(2)}) copy-start(bf16[128,256]{1,0:T(8,128)(2,1)} %param.14) | copy-start | bytes 196612
  8.9 13.7 %copy-start.13 = (f32[3456]{0:T(1024)S(1)}, f32[3456]{0:T(1024)}, u32[]{:S(2)}) copy-start(f32[3456]{0:T(1024)} %param.23) | copy-start | bytes 41476
  8.9 14.3 %copy-start.26 = (s32[128]{0:T(128)S(1)}, s32[128]{0:T(128)}, u32[]{:S(2)}) copy-start(s32[128]{0:T(128)} %param.13) | copy-start | bytes 1540
  8.9 14.3 %copy-start.15 = (f32[2,3456]{1,0:T(2,128)S(1)}, f32[2,3456]{1,0:T(2,128)}, u32[]{:S(2)}) copy-start(f32[2,3456]{1,0:T(2,128)} %param.22) | copy-start | bytes 82948
  10.6 30.3 %all-to-all-start = ((bf16[128,16,1,1,1,256]{5,1,4,3,2,0:T(8,128)(2,1)}), bf16[128,16,1,1,1,256]{5,1,4,3,2,0:T(8,128)(2,1)S(1)}, u32[]{:S(2)}, u32[]{:S(2)}) async-start(bf16[128,16,1,1,1,256]{5,1,4,3,2,0:T(8,128)(2,1)} %bitcast.2), calls=%async_computation | async-start | bytes 2097152 | tf_op jit(solution)/shard_map/all_to_all | solution.py:38
  21.8 20.1 %copy-start.9 = (bf16[16,16,128]{2,1,0:T(8,128)(2,1)S(1)}, bf16[16,16,128]{2,1,0:T(8,128)(2,1)}, u32[]{:S(2)}) copy-start(bf16[16,16,128]{2,1,0:T(8,128)(2,1)} %param.19) | copy-start | bytes 196612
  21.8 263.6 %reduce-scatter.5.cloned.1.call-start = ((), (), s32[]{:S(2)}) async-start(), calls=%async_computation.4 | async-start | bytes 7133184
  23.2 19.2 %copy-start.22 = (s32[128]{0:T(128)}, s32[128]{0:T(128)S(1)}, u32[]{:S(2)}) copy-start(s32[128]{0:T(128)S(1)} %compare_select_fusion) | copy-start | bytes 1540
  41.8 1.4 copy-start.7
  43.5 0.9 copy-start.11
  43.7 15.5 %copy-start.8 = (bf16[512,256]{0,1:T(8,128)(2,1)}, bf16[512,256]{0,1:T(8,128)(2,1)S(1)}, u32[]{:S(2)}) copy-start(bf16[512,256]{0,1:T(8,128)(2,1)S(1)} %copy.75) | copy-start | bytes 786436
  44.5 14.8 %copy-start.6 = (bf16[768,256]{0,1:T(8,128)(2,1)}, bf16[768,256]{0,1:T(8,128)(2,1)S(1)}, u32[]{:S(2)}) copy-start(bf16[768,256]{0,1:T(8,128)(2,1)S(1)} %copy.74) | copy-start | bytes 1179652
  44.5 2.7 copy-start.4
  44.5 2.7 copy-start.18
  47.2 2.7 copy-start.5
  50.5 0.8 copy-start.12
  50.6 0.8 copy-start.19
  51.4 1.8 copy-start.1
  51.4 1.8 copy-start.24
  51.4 1.8 copy-start.25
  51.4 2.4 copy-start.14
  53.8 2.8 copy-start.20
  58.4 1.8 copy-start.3
  75.1 3.9 %copy-start.2 = (bf16[1,128,27,256]{3,2,1,0:T(8,128)(2,1)S(1)}, bf16[1,128,27,256]{3,2,1,0:T(8,128)(2,1)}, u32[]{:S(2)}) copy-start(bf16[1,128,27,256]{3,2,1,0:T(8,128)(2,1)} %concatenate.29) | copy-start | bytes 5308420
  106.3 0.7 copy-start.21
  114.5 1.8 copy-start.23
  128.1 47.8 %copy-start.17 = (f32[3456]{0:T(1024)S(1)}, f32[3456]{0:T(1024)}, u32[]{:S(2)}) copy-start(f32[3456]{0:T(1024)} %get-tuple-element.21) | copy-start | bytes 41476
  128.1 47.8 %copy-start.16 = (f32[3456]{0:T(1024)S(1)}, f32[3456]{0:T(1024)}, u32[]{:S(2)}) copy-start(f32[3456]{0:T(1024)} %get-tuple-element.20) | copy-start | bytes 41476
  129.2 112.2 %all-to-all-start.1 = ((bf16[16,64,2,1,1,1,256]{6,0,2,5,4,3,1:T(8,128)(2,1)}), bf16[16,64,2,1,1,1,256]{6,0,2,5,4,3,1:T(8,128)(2,1)S(1)}, u32[]{:S(2)}, u32[]{:S(2)}) async-start(bf16[16,64,2,1,1,1,256]{6,0,2,5,4,3,1:T(8,128)(2,1)} %bitcast.47), calls=%async_computation.1 | async-start | bytes 2097152 | tf_op jit(solution)/shard_map/all_to_all | solution.py:204
Sparse Core Ops, SparseCore 0:
  106.4 178.8 reduce-scatter.4
where the time goes:
time: 296 us; the launch traced here: 294 us
  blocking collectives  110 us (37%)
  local copies, waits for them, and re-layouts  63.9 us (22%)
  waiting for transfers between devices  50.3 us (17%)
  matrix products  26.4 us (9%)
  starting transfers between devices  16.1 us (5%)
  between operations  15.3 us (5%)
  other arithmetic  12 us (4%)
    unnamed x1, blocking collectives  64 us
    psum x4, blocking collectives, one_axis_at_a_time(): shard = lax.psum(shard, axis)  41.8 us
    unnamed x2, waiting for transfers between devices  33.3 us
    all_to_all x1, waiting for transfers between devices, one_exchange(): tiles = lax.all_to_all(tiles, axis, split_axis=0, concat_axis=0, tiled=True)  17 us
    concatenate x4, local copies, waits for them, and re-layouts, body(): weight_terms = jnp.concatenate([in_term, out_term], 0)  13.1 us
    reshape x1, local copies, waits for them, and re-layouts, own_tiles(): jnp.pad(lines, ((0, 0), (0, extent * 128 - lines.shape[1])))  12.5 us
    scatter x1, local copies, waits for them, and re-layouts, block_step(): jnp.zeros(logical_grad.shape, jnp.float32).at[:, slot_of_block, :]  11.9 us
    all_to_all x1, starting transfers between devices, one_exchange(): tiles = lax.all_to_all(tiles, axis, split_axis=0, concat_axis=0, tiled=True)  11.2 us
  transfers between devices with their start and end apart: 3, of which 2 were waited for; matrix products, arithmetic and copies ran while one was open for 11% of the time, Pallas kernels for 0%

commit v1 on v0

v1 whole, which is shorter than its diff:
```python
import jax
import jax.numpy as jnp
from jax import lax
from jax.experimental import pallas as pl
from jax.experimental.pallas import tpu as pltpu
from jax.sharding import Mesh
from jax.sharding import PartitionSpec as P

BLOCK_WIDTH = 16
BLOCKS = 128
DP_REP = ("dp_0", "dp_1", "dp_2", "rep")
AXES = DP_REP
MESH = pl.DeviceIdType.MESH
DEVICES = 128
ROWS = 256
VM = pltpu.VMEM
PARTS = ((0, 96, (0, 1, 2)), (96, 176, (1, 2, 0)), (176, 256, (2, 0, 1)))
OWNED = 256


def place():
    return tuple(lax.axis_index(a) for a in AXES)


def flat(at):
    return ((at[0] * 4 + at[1]) * 4 + at[2]) * 2 + at[3]


def shifted(at, step):
    return tuple((a + (step // s) % n) % n for a, s, n in zip(at, (32, 8, 2, 1), (4, 4, 4, 2)))


def exchange_kernel(x_ref, w_ref, o_ref, t_ref, send_sem, recv_sem, tsend_sem, trecv_sem, local_sem):
    at = place()
    me = flat(at)
    own = pltpu.make_async_copy(x_ref.at[:, pl.ds(pl.multiple_of(me * ROWS, ROWS), ROWS)], o_ref.at[me], local_sem)
    own.start()

    def send(k, carry):
        to = shifted(at, (k * 37) % DEVICES)
        there = flat(to)
        pltpu.make_async_remote_copy(
            src_ref=x_ref.at[:, pl.ds(pl.multiple_of(there * ROWS, ROWS), ROWS)],
            dst_ref=o_ref.at[me], send_sem=send_sem, recv_sem=recv_sem, device_id=to, device_id_type=MESH,
        ).start()
        pltpu.make_async_remote_copy(
            src_ref=w_ref, dst_ref=t_ref.at[me], send_sem=tsend_sem, recv_sem=trecv_sem,
            device_id=to, device_id_type=MESH,
        ).start()
        return carry

    lax.fori_loop(1, DEVICES, send, 0)
    t_ref[me] = w_ref[...]
    own.wait()
    most = o_ref.at[pl.ds(0, DEVICES - 1)]
    small = t_ref.at[pl.ds(0, DEVICES - 1)]
    pltpu.make_async_copy(small, small, tsend_sem).wait()
    pltpu.make_async_copy(most, most, send_sem).wait()
    pltpu.make_async_copy(small, small, trecv_sem).wait()
    pltpu.make_async_copy(most, most, recv_sem).wait()


def exchange(pooled, weight_sum):
    any_space = pl.BlockSpec(memory_space=pl.ANY)
    vmem = pl.BlockSpec(memory_space=VM)
    dma = pltpu.SemaphoreType.DMA
    return pl.pallas_call(
        exchange_kernel,
        out_shape=(jax.ShapeDtypeStruct((DEVICES, 16, ROWS), jnp.bfloat16),
                   jax.ShapeDtypeStruct((DEVICES, 1, 128), jnp.float32)),
        in_specs=[any_space, vmem],
        out_specs=(vmem, vmem),
        scratch_shapes=[dma] * 5,
        compiler_params=pltpu.CompilerParams(has_side_effects=True),
        name="exchange",
    )(pooled, weight_sum)


def sub(ref, chosen, tail):
    return ref.at[tuple(chosen.get(d, slice(None)) for d in range(3)) + tail]


def reduce_kernel(g_ref, s_ref, out_ref, back_ref, *scratch):
    core_buf = scratch[0]
    bufs = [scratch[1 + 6 * p: 7 + 6 * p] for p in range(3)]
    (c_send, c_recv, p1_send, p1_recv, p2_send, p2_recv, p3_send, p3_recv,
     a_send, a_recv, local_sem) = scratch[19:]
    at = place()
    me = flat(at)
    core = at[3]
    other = 1 - core
    partner = at[:3] + (other,)
    steps = (2, 1, 3, 0)
    sent = []

    def remote(src, dst, ss, rs, to):
        copy = pltpu.make_async_remote_copy(
            src_ref=src, dst_ref=dst, send_sem=ss, recv_sem=rs, device_id=to, device_id_type=MESH)
        copy.start()
        sent.append(copy)
        return copy

    def moved(d, k):
        return tuple((a + k) % 4 if i == d else a for i, a in enumerate(at[:3])) + (core,)

    core_copies = {}
    for k in range(4):
        for p, (lo, hi, order) in enumerate(PARTS):
            d = order[0]
            j = (at[d] + steps[k]) % 4
            tail = (pl.ds(lo, hi - lo), slice(None))
            core_copies[p, k] = remote(
                sub(g_ref, {d: j}, (other,) + tail), sub(core_buf, {d: j}, tail),
                c_send.at[p, k], c_recv.at[p, k], partner)

    own = pltpu.make_async_copy(s_ref.at[me], back_ref.at[:, pl.ds(pl.multiple_of(me * ROWS, ROWS), ROWS)], local_sem)
    own.start()

    def send(k, carry):
        to = shifted(at, (k * 37) % DEVICES)
        pltpu.make_async_remote_copy(
            src_ref=s_ref.at[flat(to)],
            dst_ref=back_ref.at[:, pl.ds(pl.multiple_of(me * ROWS, ROWS), ROWS)],
            send_sem=a_send, recv_sem=a_recv, device_id=to, device_id_type=MESH).start()
        return carry

    half = DEVICES // 2
    lax.fori_loop(1, half, send, 0)

    def fold(p, k):
        lo, hi, order = PARTS[p]
        d = order[0]
        j = (at[d] + steps[k]) % 4
        core_copies[p, k].wait_recv()
        tail = (pl.ds(lo, hi - lo), slice(None))
        mine = sub(g_ref, {d: j}, (core,) + tail)
        got = sub(core_buf, {d: j}, tail)
        for i in range(4):
            got[i] = got[i] + mine[i]
        return got

    first = [pl.ds(0, 2), pl.ds(2, 2)]
    p1 = {}
    kept = {}
    for p in range(3):
        d = PARTS[p][2][0]
        ra, rb, rp, rm, r2, r3 = bufs[p]
        far = fold(p, 0)
        p1[p, 0] = remote(far.at[first[0]], ra, p1_send.at[p, 0], p1_recv.at[p, 0], moved(d, 1))
        p1[p, 1] = remote(far.at[first[1]], rb, p1_send.at[p, 1], p1_recv.at[p, 1], moved(d, 3))
    for p in range(3):
        d = PARTS[p][2][0]
        ra, rb, rp, rm, r2, r3 = bufs[p]
        up = fold(p, 1)
        kept[p, 1] = up
        p1[p, 2] = remote(up.at[first[1]], rp.at[first[1]], p1_send.at[p, 2], p1_recv.at[p, 2], moved(d, 1))
        down = fold(p, 2)
        kept[p, 2] = down
        p1[p, 3] = remote(down.at[first[0]], rm.at[first[0]], p1_send.at[p, 3], p1_recv.at[p, 3], moved(d, 3))
    for p in range(3):
        kept[p, 3] = fold(p, 3)
    for p in range(3):
        d = PARTS[p][2][0]
        ra, rb, rp, rm, r2, r3 = bufs[p]
        p1[p, 0].wait_recv()
        up = kept[p, 1].at[first[0]]
        up[...] = up[...] + ra[...]
        p1[p, 4] = remote(up, rp.at[first[0]], p1_send.at[p, 4], p1_recv.at[p, 4], moved(d, 1))
        p1[p, 1].wait_recv()
        down = kept[p, 2].at[first[1]]
        down[...] = down[...] + rb[...]
        p1[p, 5] = remote(down, rm.at[first[1]], p1_send.at[p, 5], p1_recv.at[p, 5], moved(d, 3))
    lax.fori_loop(half, DEVICES, send, 0)

    def select(ref, p, chosen):
        d = PARTS[p][2][0]
        dims = [i for i in range(3) if i != d]
        return ref.at[tuple(chosen.get(i, slice(None)) for i in dims)]

    p2 = {}
    for p in range(3):
        lo, hi, (d, e, f) = PARTS[p]
        ra, rb, rp, rm, r2, r3 = bufs[p]
        for i in range(2, 6):
            p1[p, i].wait_recv()
        total = kept[p, 3]
        for i in range(4):
            total[i] = (total[i].astype(jnp.float32) + rp[i].astype(jnp.float32)
                        + rm[i].astype(jnp.float32)).astype(jnp.bfloat16)
        for k in (2, 1, 3):
            p2[p, k] = remote(select(total, p, {e: (at[e] + k) % 4}), r2.at[k - 1],
                              p2_send.at[p, k - 1], p2_recv.at[p, k - 1], moved(e, k))
    p3 = {}
    held = {}
    for p in range(3):
        lo, hi, (d, e, f) = PARTS[p]
        ra, rb, rp, rm, r2, r3 = bufs[p]
        for k in (1, 2, 3):
            p2[p, k].wait_recv()
        mine = select(kept[p, 3], p, {e: at[e]})
        mine[...] = (mine[...].astype(jnp.float32) + r2[0].astype(jnp.float32) + r2[1].astype(jnp.float32)
                     + r2[2].astype(jnp.float32)).astype(jnp.bfloat16)
        held[p] = mine
        for k in (2, 1, 3):
            p3[p, k] = remote(mine.at[(at[f] + k) % 4], r3.at[k - 1],
                              p3_send.at[p, k - 1], p3_recv.at[p, k - 1], moved(f, k))
    for p in range(3):
        lo, hi, (d, e, f) = PARTS[p]
        ra, rb, rp, rm, r2, r3 = bufs[p]
        for k in (1, 2, 3):
            p3[p, k].wait_recv()
        last = held[p].at[at[f]]
        out_ref[pl.ds(lo, hi - lo), :] = (last[...].astype(jnp.float32) + r3[0].astype(jnp.float32)
                                          + r3[1].astype(jnp.float32) + r3[2].astype(jnp.float32))
    own.wait()
    for copy in sent:
        copy.wait_send()
    most = s_ref.at[pl.ds(0, DEVICES - 1)]
    pltpu.make_async_copy(most, most, a_send).wait()
    pltpu.make_async_copy(most, most, a_recv).wait()


def reduce_and_return(grads, slot_grads):
    vmem = pl.BlockSpec(memory_space=VM)
    dma = pltpu.SemaphoreType.DMA
    low = jnp.bfloat16
    buffers = [VM((4, 4, 4, OWNED, 128), low)]
    for lo, hi, _ in PARTS:
        n = hi - lo
        buffers += [VM((2, 4, n, 128), low), VM((2, 4, n, 128), low), VM((4, 4, n, 128), low),
                    VM((4, 4, n, 128), low), VM((3, 4, n, 128), low), VM((3, n, 128), low)]
    return pl.pallas_call(
        reduce_kernel,
        out_shape=(jax.ShapeDtypeStruct((OWNED, 128), jnp.float32),
                   jax.ShapeDtypeStruct((16, DEVICES * ROWS), jnp.bfloat16)),
        in_specs=[vmem, vmem],
        out_specs=(vmem, vmem),
        scratch_shapes=buffers + [dma((3, 4)), dma((3, 4)), dma((3, 6)), dma((3, 6)), dma((3, 3)), dma((3, 3)),
                                  dma((3, 3)), dma((3, 3)), dma, dma, dma],
        compiler_params=pltpu.CompilerParams(has_side_effects=True, vmem_limit_bytes=58 * 1024 * 1024),
        name="reduce_and_return",
    )(grads, slot_grads)


TILE = 432
OWNERS = 16
WIDTH = 3456
SHARE = 27
SLOT = 32


def contract(a, b, da, db):
    return lax.dot_general(a, b, (((da,), (db,)), ((), ())), preferred_element_type=jnp.float32)


def table_rows():
    rows = []
    column = 0
    for which, (count, width) in enumerate(((6, 256), (4, 64), (16, 16))):
        for t in range(count):
            rows.append((which, t, column, width))
            column += width
    return rows


def step_kernel(slot_ref, block_ref, slots_ref, dense_ref, label_ref, weight_ref, wide_ref, mid_ref, narrow_ref,
                in_ref, out_ref, vec_ref, g_ref, sg_ref,
                in_t, out_t, col, cols_ref, start, layer, low0, low1, gate0, gate1, partial, stage, bias_ref,
                owner_mask, place_mask, proj_low):
    low = jnp.bfloat16
    f32 = jnp.float32
    projections = (wide_ref, mid_ref, narrow_ref)

    for l in range(2):
        in_t[l] = in_ref[l].T
        out_t[l] = out_ref[l].T
    for i in range(WIDTH // 128):
        col[pl.ds(i * 128, 128), :] = vec_ref[:, pl.ds(i * 128, 128)].T
    row = lax.broadcasted_iota(jnp.int32, (TILE, 128), 0)
    lane = lax.broadcasted_iota(jnp.int32, (TILE, 128), 1)
    place_mask[...] = jnp.where(row % SHARE == lane, 1.0, 0.0)
    orow = lax.broadcasted_iota(jnp.int32, (OWNERS, TILE), 0)
    olane = lax.broadcasted_iota(jnp.int32, (OWNERS, TILE), 1)
    owner_mask[...] = jnp.where(olane // SHARE == orow, 1.0, 0.0).astype(low)
    for g in range(4):
        stage[g, pl.ds(TILE, 8), :] = jnp.zeros((8, 128), f32)

    def gather(b, carry):
        cols_ref[pl.ds(pl.multiple_of(b * 16, 16), 16), :] = slots_ref[slot_ref[b]]
        return carry

    lax.fori_loop(0, BLOCKS, gather, 0, unroll=8)
    start[pl.ds(0, 128), :] = dense_ref[...]
    for n, (which, t, column, width) in enumerate(table_rows()):
        start[pl.ds(128 + n * 128, 128), :] = contract(
            projections[which][t], cols_ref[pl.ds(column, width), :], 0, 0).astype(low)

    hidden0 = contract(in_t[0], start[...], 1, 0).astype(low)

    def tile(i):
        return pl.ds(pl.multiple_of(i * TILE, 16), TILE)

    def forward0(i, carry):
        at = tile(i)
        gate = contract(out_t[0, at, :], hidden0, 1, 0) + col[at, 0:1]
        gate0[at, :] = gate
        s = start[at, :].astype(f32)
        layer[at, :] = (s * gate + s).astype(low)
        return carry

    lax.fori_loop(0, WIDTH // TILE, forward0, 0)
    hidden1 = contract(in_t[1], layer[...], 1, 0).astype(low)

    def forward1(i, logit):
        at = tile(i)
        gate = contract(out_t[1, at, :], hidden1, 1, 0) + col[at, 1:2]
        gate1[at, :] = gate
        last = (start[at, :].astype(f32) * gate + layer[at, :].astype(f32)).astype(low).astype(f32)
        return logit + jnp.sum((col[at, 2:3] * last).reshape(TILE // 8, 8, ROWS), axis=0)

    logit = lax.fori_loop(0, WIDTH // TILE, forward1, jnp.zeros((8, ROWS), f32))
    logit = jnp.sum(logit, axis=0, keepdims=True)
    signal = weight_ref[...] * (jax.nn.sigmoid(logit) - label_ref[...])

    def keep_bias(l, i, gate_grad):
        sums = jnp.sum(gate_grad, axis=1, keepdims=True)
        spread = (place_mask[...] * sums).astype(low)
        bias_ref[l, pl.ds(pl.multiple_of(i * OWNERS, 16), OWNERS), :] = contract(owner_mask[...], spread, 1, 0)

    def backward1(i, carry):
        at = tile(i)
        gate_grad = start[at, :].astype(f32) * (col[at, 2:3] * signal)
        keep_bias(1, i, gate_grad)
        low1[at, :] = gate_grad.astype(low)
        return carry

    lax.fori_loop(0, WIDTH // TILE, backward1, 0)
    grad1 = contract(out_ref[1], low1[...], 1, 0).astype(low)
    last_row = lax.broadcasted_iota(jnp.int32, (SLOT, 128), 0) == SHARE

    def pack(l, i, in_term, out_term):
        for h in range(2):
            stage[h, pl.ds(0, TILE), :] = in_term[:, h * 128:(h + 1) * 128]
            stage[2 + h, pl.ds(0, TILE), :] = out_term[:, h * 128:(h + 1) * 128]
        for o in range(OWNERS):
            owner = i * OWNERS + o
            for g, group in enumerate((2 * l, 2 * l + 1, 4 + 2 * l, 5 + 2 * l)):
                piece = stage[g, pl.ds(SHARE * o, SLOT), :]
                if g == 0:
                    piece = jnp.where(last_row, bias_ref[l, pl.ds(owner, 1), :], piece)
                g_ref[owner, pl.ds(group * SLOT, SLOT), :] = piece.astype(low)

    def backward0(i, carry):
        at = tile(i)
        pack(1, i, contract(layer[at, :], grad1, 1, 1), contract(low1[at, :], hidden1, 1, 1))
        above = col[at, 2:3] * signal
        upstream = above + contract(in_ref[1, at, :], grad1, 1, 0)
        gate_grad = start[at, :].astype(f32) * upstream
        keep_bias(0, i, gate_grad)
        low0[at, :] = gate_grad.astype(low)
        partial[at, :] = gate1[at, :] * above + gate0[at, :] * upstream + upstream
        return carry

    lax.fori_loop(0, WIDTH // TILE, backward0, 0)
    grad0 = contract(out_ref[0], low0[...], 1, 0).astype(low)

    def finish(i, carry):
        at = tile(i)
        pack(0, i, contract(start[at, :], grad0, 1, 1), contract(low0[at, :], hidden0, 1, 1))
        proj_low[at, :] = (partial[at, :] + contract(in_ref[0, at, :], grad0, 1, 0)).astype(low)
        return carry

    lax.fori_loop(0, WIDTH // TILE, finish, 0)
    for n, (which, t, column, width) in enumerate(table_rows()):
        cols_ref[pl.ds(column, width), :] = contract(
            projections[which][t], proj_low[pl.ds(128 + n * 128, 128), :], 1, 0).astype(low)

    def spread(s, carry):
        sg_ref[s] = cols_ref[pl.ds(pl.multiple_of(block_ref[s] * 16, 16), 16), :]
        return carry

    lax.fori_loop(0, BLOCKS, spread, 0, unroll=8)


def local_step(slot_of_block, block_of_slot, slots, dense, labels, weights, wide, mid, narrow, cross_in, cross_out,
               vectors):
    vmem = pl.BlockSpec(memory_space=VM)
    smem = pl.BlockSpec(memory_space=pltpu.SMEM)
    low, f32 = jnp.bfloat16, jnp.float32
    wide_low = VM((WIDTH, ROWS), low)
    wide_full = VM((WIDTH, ROWS), f32)
    return pl.pallas_call(
        step_kernel,
        out_shape=(jax.ShapeDtypeStruct((DEVICES, OWNED, 128), low),
                   jax.ShapeDtypeStruct((DEVICES, 16, ROWS), low)),
        in_specs=[smem, smem] + [vmem] * 10,
        out_specs=(vmem, vmem),
        scratch_shapes=[VM((2, 256, WIDTH), low), VM((2, WIDTH, 256), low), VM((WIDTH, 8), f32),
                        VM((2048, ROWS), low), wide_low, wide_low, wide_low, wide_low,
                        wide_full, wide_full, wide_full, VM((4, TILE + 8, 128), f32), VM((2, DEVICES, 128), f32),
                        VM((OWNERS, TILE), low), VM((TILE, 128), f32), wide_low],
        compiler_params=pltpu.CompilerParams(vmem_limit_bytes=60 * 1024 * 1024),
        name="local_step",
    )(slot_of_block, block_of_slot, slots, dense, labels, weights, wide, mid, narrow, cross_in, cross_out, vectors)


def body(
    pooled,
    slot_of_block,
    dense_part,
    labels,
    sample_weight,
    proj_wide,
    proj_mid,
    proj_narrow,
    cross_in,
    cross_out,
    cross_bias,
    head_weight,
):
    batch_rows = pooled.shape[2]
    weight_sum = jnp.broadcast_to(jnp.sum(sample_weight), (1, 128))
    slots, weight_sums = exchange(pooled.reshape(BLOCK_WIDTH, batch_rows), weight_sum)
    numbers = jnp.arange(BLOCKS, dtype=jnp.int32)
    block_of_slot = jnp.sum(jnp.where(slot_of_block[None, :] == numbers[:, None], numbers[None, :], 0), 1)
    vectors = jnp.concatenate([cross_bias, head_weight[None], jnp.zeros((5, WIDTH), jnp.float32)], 0)
    grads, slot_grads = local_step(
        slot_of_block,
        block_of_slot,
        slots,
        dense_part,
        labels.astype(jnp.float32)[None],
        sample_weight[None],
        proj_wide,
        proj_mid,
        proj_narrow,
        cross_in,
        cross_out,
        vectors,
    )
    sums, returned = reduce_and_return(grads.reshape(4, 4, 4, 2, OWNED, 128), slot_grads)
    scale = batch_rows / jnp.sum(weight_sums[:, 0, 0])
    sums = sums.reshape(4, 2, SLOT, 128) * scale
    whole = jnp.moveaxis(sums[:, :, :SHARE], 1, 2).reshape(4, SHARE, 256)
    grad_bias = sums[:2, 0, SHARE, :SHARE]
    pooled_grad = (returned.astype(jnp.float32) * scale).reshape(BLOCK_WIDTH, 1, batch_rows)
    return (pooled_grad, whole[:2], jnp.swapaxes(whole[2:], 1, 2), grad_bias)


def solution(mesh):
    finer = Mesh(mesh.devices.reshape(4, 4, 4, mesh.shape["rep"]), ("dp_0", "dp_1", "dp_2", "rep"))
    return jax.shard_map(
        body,
        mesh=finer,
        in_specs=(
            P(None, DP_REP, None),
            P(),
            P(None, DP_REP),
            P(DP_REP),
            P(DP_REP),
            P(),
            P(),
            P(),
            P(),
            P(),
            P(),
            P(),
        ),
        out_specs=(
            P(None, DP_REP, None),
            P(None, DP_REP, None),
            P(None, None, DP_REP),
            P(None, DP_REP),
        ),
        check_vma=False,
    )
```

time: 296 us -> 128 us (0.43)
  blocking collectives: 110 us -> 0 us
  Pallas kernels: 0 us -> 109 us
  local copies, waits for them, and re-layouts: 63.9 us -> 7.49 us
  waiting for transfers between devices: 50.3 us -> 0 us
  matrix products: 26.4 us -> 0 us
  starting transfers between devices: 16.1 us -> 0 us
  between operations: 15.3 us -> 1.37 us
    pallas_call x0 -> x3, Pallas kernels: none -> 109 us  [the longest x1 47.8 us: reduce_and_return(): pl.pallas_call(reduce_kernel, out_shape=(jax.ShapeDtypeStruct((OWNED, 128...]
    unnamed x1 -> x0, blocking collectives: 64 us -> none
    psum x4 -> x0, blocking collectives: 41.8 us -> none  [one_axis_at_a_time(): shard = lax.psum(shard, axis)]
    unnamed x2 -> x0, waiting for transfers between devices: 33.3 us -> none
    dot_general x19 -> x0, matrix products: 26.4 us -> none  [the longest x2 7.44 us: block_step(): jnp.einsum('wk,kr->wr', cross_in[layer], hidden_grad, preferred_element_t...]
    all_to_all x2 -> x0, waiting for transfers between devices: 17 us -> none  [the longest x1 17 us: one_exchange(): tiles = lax.all_to_all(tiles, axis, split_axis=0, concat_axis=0, tiled=True)]
    all_to_all x2 -> x0, starting transfers between devices: 16.1 us -> none  [the longest x1 11.2 us: one_exchange(): tiles = lax.all_to_all(tiles, axis, split_axis=0, concat_axis=0, tiled=True)]
    concatenate x5 -> x1, local copies, waits for them, and re-layouts: 14.6 us -> 0.08 us  [body(): jnp.concatenate([cross_bias, head_weight[None], jnp.zeros((5, WIDTH), jnp...]
  transfers between devices with their start and end apart: 3 -> 0, of which waited for: 2 -> 0; matrix products, arithmetic and copies ran while one was open for 11% -> 0% of each run, Pallas kernels for 0% -> 0%
where the time goes in v1:
time: 128 us; the launch traced here: 127 us
  Pallas kernels  109 us (85%)
  other arithmetic  9.14 us (7%)
  local copies, waits for them, and re-layouts  7.49 us (6%)
  between operations  1.37 us (1%)
    pallas_call x1, Pallas kernels, reduce_and_return(): pl.pallas_call(reduce_kernel, out_shape=(jax.ShapeDtypeStruct((OWNED, 128...  47.8 us
    pallas_call x1, Pallas kernels, exchange(): pl.pallas_call(exchange_kernel, out_shape=(jax.ShapeDtypeStruct((DEVICES,...  31.7 us
    pallas_call x1, Pallas kernels, local_step(): pl.pallas_call(step_kernel, out_shape=(jax.ShapeDtypeStruct((DEVICES, OWN...  29.9 us
    unnamed x1, local copies, waits for them, and re-layouts  3.48 us

profile of v1, /device:TPU:0, one launch (start us, length us, event | category | flops | bytes accessed | tf_op | source)
XLA Modules:
  0.0 127.4 jit_solution(7980392979203406187)
XLA Ops:
  0.6 1.3 %reduce_sum.28 = f32[]{:T(128)} reduce(f32[256]{0:T(256)} %param.16, f32[]{:T(128)} %constant.0.clone.1), dimensions={0}, to_apply=%region_1.2 | reduce | flops 255 | bytes 1032 | tf_op jit(solution)/shard_map/reduce_sum | solution.py:422
  1.9 1.2 broadcast_in_dim.32.w_ref
  3.1 1.3 %select_reduce_fusion.block_ref = s32[128]{0:T(128)} fusion(s32[128]{0:T(128)} %slot_ref.1), kind=kLoop, calls=%fused_computation.5 | loop fusion | flops 49024 | bytes 1024 | tf_op jit(solution)/shard_map/reduce_sum | solution.py:425
  4.4 0.1 pad.2.clone
  4.4 1.2 convert_element_type.6
  5.7 0.7 broadcast_in_dim.35
  6.4 1.5 %maximum_maximum_fusion.vec_ref = f32[8,3456]{1,0:T(8,128)} fusion(f32[1,3456]{1,0:T(1,128)S(1)} %broadcast_in_dim.35, f32[2,3456]{1,0:T(2,128)} %param.22, f32[8]{0:T(128)S(1)} %pad.2.clone), kind=kLoop, calls=%fused_computation.2 | loop fusion | flops 55296 | bytes 152096 | tf_op jit(solution)/shard_map/concatenate | solution.py:426
  7.9 31.7 %exchange.1 = (bf16[128,16,256]{2,1,0:T(8,128)(2,1)}, f32[128,1,128]{2,1,0:T(1,128)}) custom-call(bf16[16,32768]{1,0:T(8,128)(2,1)} %bitcast.18, f32[1,128]{1,0:T(1,128)} %broadcast_in_dim.32.w_ref), custom_call_target="tpu_custom_call" | custom-call | tf_op jit(solution)/shard_map/exchange/pallas_call | solution.py:67
  39.6 1.6 %slice_reduce_fusion = f32[]{:T(128)} fusion(f32[128,1,128]{2,1,0:T(1,128)} %get-tuple-element.14), kind=kLoop, calls=%fused_computation.4 | loop fusion | flops 127 | bytes 516 | tf_op jit(solution)/shard_map/reduce_sum | solution.py:442
  41.9 29.9 %local_step.1 = (bf16[128,256,128]{2,1,0:T(8,128)(2,1)}, bf16[128,16,256]{2,1,0:T(8,128)(2,1)}) custom-call(s32[128]{0:T(128)} %slot_ref.1, s32[128]{0:T(128)} %select_reduce_fusion.block_ref, bf16[128,16,256]{2,1,0:T(8,128)(2,1)} %get-tuple-element.10.slots_ref, bf16[128,256]{1,0:T(8,128)(2,1)} %dense_ref.1, f32[1,256]{1,0:T(1,128)} %bitcast.23, ...), custom_call_target="tpu_custom_call" | custom-call | tf_op jit(solution)/shard_map/local_step/pallas_call | solution.py:392
  71.8 47.8 %reduce_and_return.1 = (f32[256,128]{1,0:T(8,128)}, bf16[16,32768]{1,0:T(8,128)(2,1)}) custom-call(bf16[4,4,4,2,256,128]{5,4,3,2,1,0:T(8,128)(2,1)} %bitcast.17, bf16[128,16,256]{2,1,0:T(8,128)(2,1)} %get-tuple-element.12.s_ref), custom_call_target="tpu_custom_call" | custom-call | tf_op jit(solution)/shard_map/reduce_and_return/pallas_call | solution.py:232
  119.6 0.9 broadcast_multiply_fusion
  120.5 0.6 slice.31
  121.2 0.7 slice.26
  121.9 0.7 slice.24
  122.6 1.4 %multiply_bitcast_fusion = f32[16,1,32768]{2,0,1:T(8,128)S(1)} fusion(bf16[16,32768]{1,0:T(8,128)(2,1)} %get-tuple-element.13, f32[]{:T(128)S(6)} %div.3), kind=kLoop, calls=%fused_computation | loop fusion | flops 1048576 | bytes 3145732 | tf_op jit(solution)/shard_map/reshape | solution.py:446
  123.9 3.5 %copy.23 = f32[16,1,32768]{2,1,0:T(1,128)} copy(f32[16,1,32768]{2,0,1:T(8,128)S(1)} %multiply_bitcast_fusion) | data formatting | bytes 4194304
  (5 shorter events, 0.1 us)

commit v2 on v0

v2 whole, which is shorter than its diff:
```python
import jax
import jax.numpy as jnp
from jax import lax
from jax.experimental import pallas as pl
from jax.experimental.pallas import tpu as pltpu
from jax.sharding import Mesh
from jax.sharding import PartitionSpec as P

BLOCK_WIDTH = 16
BLOCKS = 128
DP_REP = ("dp_0", "dp_1", "dp_2", "rep")
AXES = DP_REP
MESH = pl.DeviceIdType.MESH
DEVICES = 128
ROWS = 256
TILE = 432
TILES = 8
OWNERS = 16
WIDTH = 3456
SHARE = 27
SLOT = 32
OWNED = 128
VM = pltpu.VMEM
PARTS = (
    ((0, 32, (0, 1, 2)), (32, 80, (1, 2, 0)), (80, 128, (2, 0, 1))),
    ((0, 48, (0, 1, 2)), (48, 96, (1, 2, 0)), (96, 128, (2, 0, 1))),
)
HALVES = (pl.ds(0, 2), pl.ds(2, 2))


def place():
    return tuple(lax.axis_index(a) for a in AXES)


def flat(at):
    return ((at[0] * 4 + at[1]) * 4 + at[2]) * 2 + at[3]


def shifted(at, step):
    return tuple((a + (step // s) % n) % n for a, s, n in zip(at, (32, 8, 2, 1), (4, 4, 4, 2)))


def columns(device):
    return pl.ds(pl.multiple_of(device * ROWS, ROWS), ROWS)


def contract(a, b, da, db):
    return lax.dot_general(a, b, (((da,), (db,)), ((), ())), preferred_element_type=jnp.float32)


def table_rows():
    rows = []
    column = 0
    for which, (count, width) in enumerate(((6, 256), (4, 64), (16, 16))):
        for t in range(count):
            rows.append((which, t, column, width))
            column += width
    return rows


def sub(ref, chosen, tail):
    return ref.at[tuple(chosen.get(d, slice(None)) for d in range(3)) + tail]


class Reduction:
    def __init__(self, layer, at, grads, core_buf, bufs, sems, remote):
        self.layer, self.at, self.core = layer, at, at[3]
        self.grads, self.core_buf, self.bufs, self.sems = grads, core_buf, bufs, sems
        self.remote = remote
        self.one, self.two, self.three, self.kept = {}, {}, {}, {}

    def moved(self, d, k):
        return tuple((a + k) % 4 if i == d else a for i, a in enumerate(self.at[:3])) + (self.core,)

    def send_tile(self, i):
        there = pl.ds(2 * (i % 2), 2)
        self.remote(
            self.grads.at[i // 2, there, :, 1 - self.core], self.core_buf.at[i // 2, there],
            self.sems["core_send"].at[self.layer], self.sems["core_recv"].at[self.layer],
            self.at[:3] + (1 - self.core,), False)

    def wait_core(self, which):
        pltpu.make_async_copy(self.core_buf, self.core_buf, self.sems[which].at[self.layer]).wait()

    def step(self, which, p, n, src, dst, d, k):
        return self.remote(src, dst, self.sems[which + "_send"].at[self.layer, p, n],
                           self.sems[which + "_recv"].at[self.layer, p, n], self.moved(d, k), True)

    def first(self):
        self.wait_core("core_recv")

        def fold(b, carry):
            x, z = b // 4, b % 4
            for y in range(4):
                self.core_buf[x, z, y] = self.core_buf[x, z, y] + self.grads[x, z, y, self.core]
            return carry

        lax.fori_loop(0, 16, fold, 0)
        for p, (lo, hi, (d, _, _)) in enumerate(PARTS[self.layer]):
            tail = (pl.ds(lo, hi - lo), slice(None))
            for k in range(4):
                self.kept[p, k] = sub(self.core_buf, {d: (self.at[d] + k) % 4}, tail)
            ra, rb = self.bufs[p][:2]
            self.one[p, 0] = self.step("one", p, 0, self.kept[p, 2].at[HALVES[0]], ra, d, 1)
            self.one[p, 1] = self.step("one", p, 1, self.kept[p, 2].at[HALVES[1]], rb, d, 3)
        for p, (lo, hi, (d, _, _)) in enumerate(PARTS[self.layer]):
            rp, rm = self.bufs[p][2:4]
            self.one[p, 2] = self.step(
                "one", p, 2, self.kept[p, 1].at[HALVES[1]], rp.at[HALVES[1]], d, 1)
            self.one[p, 3] = self.step(
                "one", p, 3, self.kept[p, 3].at[HALVES[0]], rm.at[HALVES[0]], d, 3)

    def middle(self):
        for p, (lo, hi, (d, _, _)) in enumerate(PARTS[self.layer]):
            ra, rb, rp, rm = self.bufs[p][:4]
            self.one[p, 0].wait_recv()
            up = self.kept[p, 1].at[HALVES[0]]
            up[...] = up[...] + ra[...]
            self.one[p, 4] = self.step("one", p, 4, up, rp.at[HALVES[0]], d, 1)
            self.one[p, 1].wait_recv()
            down = self.kept[p, 3].at[HALVES[1]]
            down[...] = down[...] + rb[...]
            self.one[p, 5] = self.step("one", p, 5, down, rm.at[HALVES[1]], d, 3)

    def second(self):
        f32 = jnp.float32
        for p, (lo, hi, (d, e, f)) in enumerate(PARTS[self.layer]):
            rp, rm, r2 = self.bufs[p][2:5]
            for n in range(2, 6):
                self.one[p, n].wait_recv()
            total = self.kept[p, 0]
            for i in range(4):
                total[i] = (total[i].astype(f32) + rp[i].astype(f32) + rm[i].astype(f32)).astype(jnp.bfloat16)
            for k in (2, 1, 3):
                self.two[p, k] = self.step(
                    "two", p, k - 1, self.pick(p, {e: (self.at[e] + k) % 4}), r2.at[k - 1], e, k)

    def pick(self, p, chosen):
        d = PARTS[self.layer][p][2][0]
        return self.kept[p, 0].at[tuple(chosen.get(i, slice(None)) for i in range(3) if i != d)]

    def third(self):
        f32 = jnp.float32
        self.held = {}
        for p, (lo, hi, (d, e, f)) in enumerate(PARTS[self.layer]):
            r2, r3 = self.bufs[p][4:6]
            for k in (1, 2, 3):
                self.two[p, k].wait_recv()
            mine = self.pick(p, {e: self.at[e]})
            mine[...] = (mine[...].astype(f32) + r2[0].astype(f32) + r2[1].astype(f32)
                         + r2[2].astype(f32)).astype(jnp.bfloat16)
            self.held[p] = mine
            for k in (2, 1, 3):
                self.three[p, k] = self.step(
                    "three", p, k - 1, mine.at[(self.at[f] + k) % 4], r3.at[k - 1], f, k)

    def last(self, out_ref):
        f32 = jnp.float32
        for p, (lo, hi, (d, e, f)) in enumerate(PARTS[self.layer]):
            r3 = self.bufs[p][5]
            for k in (1, 2, 3):
                self.three[p, k].wait_recv()
            out_ref[self.layer, pl.ds(lo, hi - lo), :] = (
                self.held[p].at[self.at[f]][...].astype(f32) + r3[0].astype(f32) + r3[1].astype(f32)
                + r3[2].astype(f32))


SEMS = (("core_send", (2,)), ("core_recv", (2,)), ("one_send", (2, 3, 6)), ("one_recv", (2, 3, 6)),
        ("two_send", (2, 3, 3)), ("two_recv", (2, 3, 3)), ("three_send", (2, 3, 3)), ("three_recv", (2, 3, 3)),
        ("fwd_send", ()), ("fwd_recv", ()), ("sum_send", ()), ("sum_recv", ()), ("back_send", ()),
        ("back_recv", ()), ("local", (6,)))


def whole_kernel(slot_ref, block_ref, x_ref, dense_ref, label_ref, weight_ref, wide_ref, mid_ref, narrow_ref,
                 in_hbm, out_hbm, bias_in, head_ref, sums_ref, back_ref, total_ref,
                 slots_ref, w_ref, t_ref, in_ref, out_ref, in_t, out_t, vec_ref, col, cols_ref, sg_ref, lg_ref, start, layer,
                 low0, low1, gate0, gate1, stage, bias_ref, owner_mask, place_mask, *rest):
    low = jnp.bfloat16
    f32 = jnp.float32
    projections = (wide_ref, mid_ref, narrow_ref)
    grads, core_bufs, rest = rest[:2], rest[2:4], rest[4:]
    rs_bufs = [[rest[(l * 3 + p) * 6:(l * 3 + p + 1) * 6] for p in range(3)] for l in range(2)]
    sems = {name: sem for (name, _), sem in zip(SEMS, rest[36:])}
    at = place()
    me = flat(at)
    sent = []

    def remote(src, dst, ss, rs, to, keep):
        copy = pltpu.make_async_remote_copy(
            src_ref=src, dst_ref=dst, send_sem=ss, recv_sem=rs, device_id=to, device_id_type=MESH)
        copy.start()
        if keep:
            sent.append(copy)
        return copy

    barrier = pltpu.get_barrier_semaphore()

    def greet(k, carry):
        pl.semaphore_signal(barrier, inc=1, device_id=shifted(at, k), device_id_type=MESH)
        return carry

    lax.fori_loop(1, DEVICES, greet, 0)
    loads = []
    for l in range(2):
        loads.append(pltpu.make_async_copy(in_hbm.at[l], in_ref.at[l], sems["local"].at[l]))
        loads.append(pltpu.make_async_copy(out_hbm.at[l], out_ref.at[l], sems["local"].at[2 + l]))
    for load in loads:
        load.start()
    own = pltpu.make_async_copy(x_ref.at[:, columns(me)], slots_ref.at[me], sems["local"].at[4])
    own.start()
    local_sum = jnp.sum(weight_ref[...], axis=1, keepdims=True)
    w_ref[...] = jnp.broadcast_to(local_sum, (1, 128))
    t_ref[me] = jnp.broadcast_to(local_sum, (1, 128))
    pl.semaphore_wait(barrier, DEVICES - 1)

    def send_forward(k, carry):
        to = shifted(at, (k * 37) % DEVICES)
        remote(x_ref.at[:, columns(flat(to))], slots_ref.at[me], sems["fwd_send"], sems["fwd_recv"], to, False)
        return carry

    def send_sum(k, carry):
        to = shifted(at, (k * 37) % DEVICES)
        remote(w_ref, t_ref.at[me], sems["sum_send"], sems["sum_recv"], to, False)
        return carry

    lax.fori_loop(1, DEVICES, send_forward, 0)
    lax.fori_loop(1, DEVICES, send_sum, 0)

    row = lax.broadcasted_iota(jnp.int32, (TILE, 128), 0)
    lane = lax.broadcasted_iota(jnp.int32, (TILE, 128), 1)
    place_mask[...] = jnp.where(row % SHARE == lane, 1.0, 0.0)
    owner_row = lax.broadcasted_iota(jnp.int32, (OWNERS, TILE), 0)
    owner_lane = lax.broadcasted_iota(jnp.int32, (OWNERS, TILE), 1)
    owner_mask[...] = jnp.where(owner_lane // SHARE == owner_row, 1.0, 0.0).astype(low)
    for g in range(4):
        stage[g, pl.ds(TILE, 8), :] = jnp.zeros((8, 128), f32)
    vec_ref[...] = jnp.zeros(vec_ref.shape, f32)
    vec_ref[pl.ds(0, 2), :] = bias_in[...]
    vec_ref[pl.ds(2, 1), :] = head_ref[...]
    for i in range(WIDTH // 128):
        col[pl.ds(i * 128, 128), :] = vec_ref[:, pl.ds(i * 128, 128)].T
    start[pl.ds(0, 128), :] = dense_ref[...]
    for load in loads:
        load.wait()
    for l in range(2):
        in_t[l] = in_ref[l].T
        out_t[l] = out_ref[l].T
    own.wait()
    most = slots_ref.at[pl.ds(0, DEVICES - 1)]
    pltpu.make_async_copy(most, most, sems["fwd_recv"]).wait()

    def gather(b, carry):
        cols_ref[pl.ds(pl.multiple_of(b * 16, 16), 16), :] = slots_ref[slot_ref[b]]
        return carry

    lax.fori_loop(0, BLOCKS, gather, 0, unroll=8)
    for n, (which, t, column, width) in enumerate(table_rows()):
        start[pl.ds(128 + n * 128, 128), :] = contract(
            projections[which][t], cols_ref[pl.ds(column, width), :], 0, 0).astype(low)

    hidden0 = contract(in_t[0], start[...], 1, 0).astype(low)

    def tile(i):
        return pl.ds(pl.multiple_of(i * TILE, 16), TILE)

    def forward0(i, carry):
        here = tile(i)
        gate = contract(out_t[0, here, :], hidden0, 1, 0) + col[here, 0:1]
        gate0[here, :] = gate
        s = start[here, :].astype(f32)
        layer[here, :] = (s * gate + s).astype(low)
        return carry

    lax.fori_loop(0, TILES, forward0, 0)
    hidden1 = contract(in_t[1], layer[...], 1, 0).astype(low)

    def forward1(i, logit):
        here = tile(i)
        gate = contract(out_t[1, here, :], hidden1, 1, 0) + col[here, 1:2]
        gate1[here, :] = gate
        last = (start[here, :].astype(f32) * gate + layer[here, :].astype(f32)).astype(low).astype(f32)
        return logit + jnp.sum((col[here, 2:3] * last).reshape(TILE // 8, 8, ROWS), axis=0)

    logit = lax.fori_loop(0, TILES, forward1, jnp.zeros((8, ROWS), f32))
    logit = jnp.sum(logit, axis=0, keepdims=True)
    signal = weight_ref[...] * (jax.nn.sigmoid(logit) - label_ref[...].astype(f32))

    def keep_bias(l, i, gate_grad):
        sums = jnp.sum(gate_grad, axis=1, keepdims=True)
        spread = (place_mask[...] * sums).astype(low)
        bias_ref[l, pl.ds(pl.multiple_of(i * OWNERS, 16), OWNERS), :] = contract(owner_mask[...], spread, 1, 0)

    def backward1(i, carry):
        here = tile(i)
        gate_grad = start[here, :].astype(f32) * (col[here, 2:3] * signal)
        keep_bias(1, i, gate_grad)
        low1[here, :] = gate_grad.astype(low)
        return carry

    lax.fori_loop(0, TILES, backward1, 0)
    grad1 = contract(out_ref[1], low1[...], 1, 0).astype(low)
    bias_row = lax.broadcasted_iota(jnp.int32, (SLOT, 128), 0) == SHARE
    reductions = [
        Reduction(l, at, grads[l], core_bufs[l], rs_bufs[l], sems, remote) for l in range(2)]

    def pack(l, i, in_term, out_term):
        for h in range(2):
            stage[h, pl.ds(0, TILE), :] = in_term[:, h * 128:(h + 1) * 128]
            stage[2 + h, pl.ds(0, TILE), :] = out_term[:, h * 128:(h + 1) * 128]
        for o in range(OWNERS):
            for g in range(4):
                piece = stage[g, pl.ds(SHARE * o, SLOT), :]
                if g == 0:
                    piece = jnp.where(bias_row, bias_ref[l, pl.ds(i * OWNERS + o, 1), :], piece)
                grads[l][i // 2, 2 * (i % 2) + o // 8, (o // 2) % 4, o % 2, pl.ds(g * SLOT, SLOT), :] = (
                    piece.astype(low))

        @pl.when(i > 0)
        def _():
            reductions[l].send_tile(i - 1)

    def backward0(i, carry):
        here = tile(i)
        pack(1, i, contract(layer[here, :], grad1, 1, 1), contract(low1[here, :], hidden1, 1, 1))
        above = col[here, 2:3] * signal
        upstream = above + contract(in_ref[1, here, :], grad1, 1, 0)
        gate_grad = start[here, :].astype(f32) * upstream
        keep_bias(0, i, gate_grad)
        low0[here, :] = gate_grad.astype(low)
        gate0[here, :] = gate1[here, :] * above + gate0[here, :] * upstream + upstream
        return carry

    lax.fori_loop(0, TILES, backward0, 0)
    reductions[1].send_tile(TILES - 1)
    grad0 = contract(out_ref[0], low0[...], 1, 0).astype(low)
    reductions[1].first()

    def finish(i, carry):
        here = tile(i)
        low1[here, :] = (gate0[here, :] + contract(in_ref[0, here, :], grad0, 1, 0)).astype(low)
        return carry

    lax.fori_loop(0, TILES, finish, 0)
    for n, (which, t, column, width) in enumerate(table_rows()):
        lg_ref[pl.ds(column // 16, width // 16)] = contract(
            projections[which][t], low1[pl.ds(128 + n * 128, 128), :], 1, 0).astype(low).reshape(
                width // 16, 16, ROWS)

    def spread(s, carry):
        sg_ref[s] = lg_ref[block_ref[s]]
        return carry

    lax.fori_loop(0, BLOCKS, spread, 0, unroll=8)
    reductions[1].middle()

    own_back = pltpu.make_async_copy(sg_ref.at[me], back_ref.at[:, columns(me)], sems["local"].at[5])
    own_back.start()

    def send_back(k, carry):
        to = shifted(at, (k * 37) % DEVICES)
        remote(sg_ref.at[flat(to)], back_ref.at[:, columns(me)], sems["back_send"], sems["back_recv"], to, False)
        return carry

    lax.fori_loop(1, 64, send_back, 0)

    def terms0(i, carry):
        here = tile(i)
        pack(0, i, contract(start[here, :], grad0, 1, 1), contract(low0[here, :], hidden0, 1, 1))
        return carry

    lax.fori_loop(0, TILES, terms0, 0)
    reductions[0].send_tile(TILES - 1)
    reductions[1].second()
    reductions[0].first()
    lax.fori_loop(64, 96, send_back, 0)
    reductions[1].third()
    reductions[0].middle()
    lax.fori_loop(96, DEVICES, send_back, 0)
    reductions[1].last(sums_ref)
    reductions[0].second()
    small = t_ref.at[pl.ds(0, DEVICES - 1)]
    pltpu.make_async_copy(small, small, sems["sum_recv"]).wait()
    total_ref[...] = jnp.sum(t_ref[...], axis=0)
    reductions[0].third()
    reductions[0].last(sums_ref)

    own_back.wait()
    for copy in sent:
        copy.wait_send()
    for reduction in reductions:
        reduction.wait_core("core_send")
    pltpu.make_async_copy(small, small, sems["sum_send"]).wait()
    pltpu.make_async_copy(most, most, sems["fwd_send"]).wait()
    pltpu.make_async_copy(most, most, sems["back_send"]).wait()
    pltpu.make_async_copy(most, most, sems["back_recv"]).wait()


def whole(slot_of_block, block_of_slot, pooled, dense, labels, weights, wide, mid, narrow, cross_in, cross_out, bias,
          head):
    vmem = pl.BlockSpec(memory_space=VM)
    smem = pl.BlockSpec(memory_space=pltpu.SMEM)
    hbm = pl.BlockSpec(memory_space=pl.ANY)
    low, f32 = jnp.bfloat16, jnp.float32
    activation = VM((WIDTH, ROWS), low)
    full = VM((WIDTH, ROWS), f32)
    scratch = [
        VM((DEVICES, 16, ROWS), low), VM((1, 128), f32), VM((DEVICES, 1, 128), f32),
        VM((2, WIDTH, 256), low), VM((2, 256, WIDTH), low), VM((2, 256, WIDTH), low), VM((2, WIDTH, 256), low),
        VM((8, WIDTH), f32), VM((WIDTH, 8), f32), VM((2048, ROWS), low), VM((DEVICES, 16, ROWS), low),
        VM((DEVICES, 16, ROWS), low),
        activation, activation, activation, activation, full, full,
        VM((4, TILE + 8, 128), f32), VM((2, DEVICES, 128), f32), VM((OWNERS, TILE), low), VM((TILE, 128), f32),
    ]
    scratch += [VM((4, 4, 4, 2, OWNED, 128), low)] * 2 + [VM((4, 4, 4, OWNED, 128), low)] * 2
    for l in range(2):
        for lo, hi, _ in PARTS[l]:
            n = hi - lo
            scratch += [VM((2, 4, n, 128), low), VM((2, 4, n, 128), low), VM((4, 4, n, 128), low),
                        VM((4, 4, n, 128), low), VM((3, 4, n, 128), low), VM((3, n, 128), low)]
    scratch += [pltpu.SemaphoreType.DMA(shape) if shape else pltpu.SemaphoreType.DMA for _, shape in SEMS]
    return pl.pallas_call(
        whole_kernel,
        out_shape=(jax.ShapeDtypeStruct((2, OWNED, 128), f32),
                   jax.ShapeDtypeStruct((16, DEVICES * ROWS), low),
                   jax.ShapeDtypeStruct((1, 128), f32)),
        in_specs=[smem, smem, hbm] + [vmem] * 6 + [hbm, hbm, vmem, vmem],
        out_specs=(vmem, vmem, vmem),
        scratch_shapes=scratch,
        compiler_params=pltpu.CompilerParams(
            has_side_effects=True, collective_id=0, vmem_limit_bytes=60 * 1024 * 1024),
        name="whole",
    )(slot_of_block, block_of_slot, pooled, dense, labels, weights, wide, mid, narrow, cross_in, cross_out, bias, head)


def body(
    pooled,
    slot_of_block,
    dense_part,
    labels,
    sample_weight,
    proj_wide,
    proj_mid,
    proj_narrow,
    cross_in,
    cross_out,
    cross_bias,
    head_weight,
):
    batch_rows = pooled.shape[2]
    numbers = jnp.arange(BLOCKS, dtype=jnp.int32)
    block_of_slot = jnp.sum(jnp.where(slot_of_block[None, :] == numbers[:, None], numbers[None, :], 0), 1)
    sums, returned, total = whole(
        slot_of_block,
        block_of_slot,
        pooled.reshape(BLOCK_WIDTH, batch_rows),
        dense_part,
        labels[None],
        sample_weight[None],
        proj_wide,
        proj_mid,
        proj_narrow,
        cross_in,
        cross_out,
        cross_bias,
        head_weight[None],
    )
    scale = batch_rows / total[0, 0]
    sums = sums.reshape(2, 2, 2, SLOT, 128) * scale
    whole_sums = jnp.moveaxis(sums[:, :, :, :SHARE], 2, 3).reshape(2, 2, SHARE, 256)
    grad_bias = sums[:, 0, 0, SHARE, :SHARE]
    pooled_grad = (returned.astype(jnp.float32) * scale).reshape(BLOCK_WIDTH, 1, batch_rows)
    return (pooled_grad, whole_sums[:, 0], jnp.swapaxes(whole_sums[:, 1], 1, 2), grad_bias)


def solution(mesh):
    finer = Mesh(mesh.devices.reshape(4, 4, 4, mesh.shape["rep"]), ("dp_0", "dp_1", "dp_2", "rep"))
    return jax.shard_map(
        body,
        mesh=finer,
        in_specs=(
            P(None, DP_REP, None),
            P(),
            P(None, DP_REP),
            P(DP_REP),
            P(DP_REP),
            P(),
            P(),
            P(),
            P(),
            P(),
            P(),
            P(),
        ),
        out_specs=(
            P(None, DP_REP, None),
            P(None, DP_REP, None),
            P(None, None, DP_REP),
            P(None, DP_REP),
        ),
        check_vma=False,
    )
```

time: 296 us -> 100 us (0.34)
  blocking collectives: 110 us -> 0 us
  Pallas kernels: 0 us -> 89 us
  local copies, waits for them, and re-layouts: 63.9 us -> 6.24 us
  waiting for transfers between devices: 50.3 us -> 0 us
  matrix products: 26.4 us -> 0 us
  starting transfers between devices: 16.1 us -> 0 us
  between operations: 15.3 us -> 1.32 us
  other arithmetic: 12 us -> 3.56 us
    pallas_call x0 -> x1, Pallas kernels: none -> 89 us  [whole(): pl.pallas_call(whole_kernel, out_shape=(jax.ShapeDtypeStruct((2, OWNED, 1...]
    unnamed x1 -> x0, blocking collectives: 64 us -> none
    psum x4 -> x0, blocking collectives: 41.8 us -> none  [one_axis_at_a_time(): shard = lax.psum(shard, axis)]
    unnamed x2 -> x0, waiting for transfers between devices: 33.3 us -> none
    dot_general x19 -> x0, matrix products: 26.4 us -> none  [the longest x2 7.44 us: block_step(): jnp.einsum('wk,kr->wr', cross_in[layer], hidden_grad, preferred_element_t...]
    all_to_all x2 -> x0, waiting for transfers between devices: 17 us -> none  [the longest x1 17 us: one_exchange(): tiles = lax.all_to_all(tiles, axis, split_axis=0, concat_axis=0, tiled=True)]
    all_to_all x2 -> x0, starting transfers between devices: 16.1 us -> none  [the longest x1 11.2 us: one_exchange(): tiles = lax.all_to_all(tiles, axis, split_axis=0, concat_axis=0, tiled=True)]
    concatenate x5 -> x0, local copies, waits for them, and re-layouts: 14.6 us -> none  [the longest x4 13.1 us: body(): weight_terms = jnp.concatenate([in_term, out_term], 0)]
  transfers between devices with their start and end apart: 3 -> 0, of which waited for: 2 -> 0; matrix products, arithmetic and copies ran while one was open for 11% -> 0% of each run, Pallas kernels for 0% -> 0%
where the time goes in v2:
time: 100 us
  Pallas kernels  89 us (89%)
  local copies, waits for them, and re-layouts  6.24 us (6%)
  other arithmetic  3.56 us (4%)
  between operations  1.32 us (1%)
    pallas_call x1, Pallas kernels, whole(): pl.pallas_call(whole_kernel, out_shape=(jax.ShapeDtypeStruct((2, OWNED, 1...  89 us
    unnamed x1, local copies, waits for them, and re-layouts  3.48 us

profile of v2, /device:TPU:0, one launch (start us, length us, event | category | flops | bytes accessed | tf_op | source)
XLA Modules:
  0.0 100.2 jit_solution(2772078140872629889)
XLA Ops:
  0.6 1.3 %select_reduce_fusion.block_ref = s32[128]{0:T(128)} fusion(s32[128]{0:T(128)} %slot_ref.1), kind=kLoop, calls=%fused_computation.3 | loop fusion | flops 49024 | bytes 1024 | tf_op jit(solution)/shard_map/reduce_sum | solution.py:451
  1.9 1.3 %broadcast_in_dim.28.head_ref = f32[1,3456]{1,0:T(1,128)} reshape(f32[3456]{0:T(1024)} %param.23) | data formatting | bytes 27648 | tf_op jit(solution)/shard_map/broadcast_in_dim | solution.py:465
  3.2 89.0 %whole.1 = (f32[2,128,128]{2,1,0:T(8,128)}, bf16[16,32768]{1,0:T(8,128)(2,1)}, f32[1,128]{1,0:T(1,128)}) custom-call(s32[128]{0:T(128)} %slot_ref.1, s32[128]{0:T(128)} %select_reduce_fusion.block_ref, bf16[16,32768]{1,0:T(8,128)(2,1)} %bitcast.21, bf16[128,256]{1,0:T(8,128)(2,1)} %dense_ref.1, s32[1,256]{1,0:T(1,128)} %bitcast.24, f32[1,256]{1,0:T(1,128)} %bitcast.25, ...), custom_call_target="tpu_custom_call" | custom-call | tf_op jit(solution)/shard_map/whole/pallas_call | solution.py:421
  93.0 0.9 broadcast_multiply_fusion
  93.9 0.6 slice.23
  94.4 0.1 copy.19
  94.5 0.1 reshape.25
  94.7 0.6 slice_bitcast_fusion.1
  95.3 1.4 %multiply_bitcast_fusion = f32[16,1,32768]{2,0,1:T(8,128)S(1)} fusion(bf16[16,32768]{1,0:T(8,128)(2,1)} %get-tuple-element.7, f32[]{:T(128)} %bitcast.3), kind=kLoop, calls=%fused_computation | loop fusion | flops 1048576 | bytes 3145732 | tf_op jit(solution)/shard_map/reshape | solution.py:471
  96.7 3.5 %copy.21 = f32[16,1,32768]{2,1,0:T(1,128)} copy(f32[16,1,32768]{2,0,1:T(8,128)S(1)} %multiply_bitcast_fusion) | data formatting | bytes 4194304
  (1 shorter events, 0.0 us)

commit v3 on v2

--- a/solution.py
+++ b/solution.py
@@ -8,6 +8,7 @@
 
 BLOCK_WIDTH = 16
 BLOCKS = 128
+BATCH_ROWS = 32768
 DP_REP = ("dp_0", "dp_1", "dp_2", "rep")
 AXES = DP_REP
 MESH = pl.DeviceIdType.MESH
@@ -25,6 +26,8 @@
     ((0, 32, (0, 1, 2)), (32, 80, (1, 2, 0)), (80, 128, (2, 0, 1))),
     ((0, 48, (0, 1, 2)), (48, 96, (1, 2, 0)), (96, 128, (2, 0, 1))),
 )
+TURN_X = (0, 1, 2, 3, 1, 2, 3, 0)
+TURN_Z = (0, 2, 1, 3, 3, 1, 0, 2)
 HALVES = (pl.ds(0, 2), pl.ds(2, 2))
 
 
@@ -34,10 +37,6 @@
 
 def flat(at):
     return ((at[0] * 4 + at[1]) * 4 + at[2]) * 2 + at[3]
-
-
-def shifted(at, step):
-    return tuple((a + (step // s) % n) % n for a, s, n in zip(at, (32, 8, 2, 1), (4, 4, 4, 2)))
 
 
 def columns(device):
@@ -168,7 +167,7 @@
 SEMS = (("core_send", (2,)), ("core_recv", (2,)), ("one_send", (2, 3, 6)), ("one_recv", (2, 3, 6)),
         ("two_send", (2, 3, 3)), ("two_recv", (2, 3, 3)), ("three_send", (2, 3, 3)), ("three_recv", (2, 3, 3)),
         ("fwd_send", ()), ("fwd_recv", ()), ("sum_send", ()), ("sum_recv", ()), ("back_send", ()),
-        ("back_recv", ()), ("local", (6,)))
+        ("back_recv", ()), ("local", (7,)))
 
 
 def whole_kernel(slot_ref, block_ref, x_ref, dense_ref, label_ref, weight_ref, wide_ref, mid_ref, narrow_ref,
@@ -180,7 +179,8 @@
     projections = (wide_ref, mid_ref, narrow_ref)
     grads, core_bufs, rest = rest[:2], rest[2:4], rest[4:]
     rs_bufs = [[rest[(l * 3 + p) * 6:(l * 3 + p + 1) * 6] for p in range(3)] for l in range(2)]
-    sems = {name: sem for (name, _), sem in zip(SEMS, rest[36:])}
+    sems = {name: sem for (name, _), sem in zip(SEMS, rest[36:-1])}
+    sems["round"] = rest[-1]
     at = place()
     me = flat(at)
     sent = []
@@ -195,11 +195,11 @@
 
     barrier = pltpu.get_barrier_semaphore()
 
-    def greet(k, carry):
-        pl.semaphore_signal(barrier, inc=1, device_id=shifted(at, k), device_id_type=MESH)
-        return carry
-
-    lax.fori_loop(1, DEVICES, greet, 0)
+    lines = [[tuple((a + k) % 4 if i == d else a for i, a in enumerate(at[:3])) + at[3:] for k in (1, 2, 3)]
+             for d in range(3)]
+    near = [at[:3] + (1 - at[3],)] + lines[0] + lines[1] + lines[2]
+    for device in near:
+        pl.semaphore_signal(barrier, inc=1, device_id=device, device_id_type=MESH)
     loads = []
     for l in range(2):
         loads.append(pltpu.make_async_copy(in_hbm.at[l], in_ref.at[l], sems["local"].at[l]))
@@ -211,20 +211,40 @@
     local_sum = jnp.sum(weight_ref[...], axis=1, keepdims=True)
     w_ref[...] = jnp.broadcast_to(local_sum, (1, 128))
     t_ref[me] = jnp.broadcast_to(local_sum, (1, 128))
-    pl.semaphore_wait(barrier, DEVICES - 1)
-
-    def send_forward(k, carry):
-        to = shifted(at, (k * 37) % DEVICES)
+    pl.semaphore_wait(barrier, len(near))
+    for d in (2, 1, 0):
+        for device in lines[d]:
+            pl.semaphore_signal(sems["round"].at[d], inc=1, device_id=device, device_id_type=MESH)
+        pl.semaphore_wait(sems["round"].at[d], 3)
+
+    def to_all(lo, hi, send):
+        def some(i, carry):
+            xs = [(at[0] + i + q) % 4 for q in range(4)]
+            zs = [(at[1] + i // 4 + q) % 4 for q in range(4)]
+            for n in range(8):
+                to = (xs[TURN_X[n]], zs[TURN_Z[n]], ys[n // 2], cores[n % 2])
+                if n == 0:
+                    @pl.when(i > 0)
+                    def _():
+                        send(to)
+                else:
+                    send(to)
+            return carry
+
+        ys = [(at[2] + q) % 4 for q in range(4)]
+        cores = [at[3], 1 - at[3]]
+        lax.fori_loop(lo, hi, some, 0)
+
+    def send_forward(to):
         remote(x_ref.at[:, columns(flat(to))], slots_ref.at[me], sems["fwd_send"], sems["fwd_recv"], to, False)
-        return carry
-
-    def send_sum(k, carry):
-        to = shifted(at, (k * 37) % DEVICES)
+
+    def send_sum(to):
         remote(w_ref, t_ref.at[me], sems["sum_send"], sems["sum_recv"], to, False)
-        return carry
-
-    lax.fori_loop(1, DEVICES, send_forward, 0)
-    lax.fori_loop(1, DEVICES, send_sum, 0)
+
+    def send_back(to):
+        remote(sg_ref.at[flat(to)], back_ref.at[:, columns(me)], sems["back_send"], sems["back_recv"], to, False)
+
+    to_all(0, 16, send_forward)
 
     row = lax.broadcasted_iota(jnp.int32, (TILE, 128), 0)
     lane = lax.broadcasted_iota(jnp.int32, (TILE, 128), 1)
@@ -236,7 +256,8 @@
         stage[g, pl.ds(TILE, 8), :] = jnp.zeros((8, 128), f32)
     vec_ref[...] = jnp.zeros(vec_ref.shape, f32)
     vec_ref[pl.ds(0, 2), :] = bias_in[...]
-    vec_ref[pl.ds(2, 1), :] = head_ref[...]
+    for i in range(WIDTH // 128):
+        vec_ref[2, pl.ds(i * 128, 128)] = head_ref[pl.ds(i * 128, 128)]
     for i in range(WIDTH // 128):
         col[pl.ds(i * 128, 128), :] = vec_ref[:, pl.ds(i * 128, 128)].T
     start[pl.ds(0, 128), :] = dense_ref[...]
@@ -245,6 +266,7 @@
     for l in range(2):
         in_t[l] = in_ref[l].T
         out_t[l] = out_ref[l].T
+    to_all(0, 16, send_sum)
     own.wait()
     most = slots_ref.at[pl.ds(0, DEVICES - 1)]
     pltpu.make_async_copy(most, most, sems["fwd_recv"]).wait()
@@ -351,17 +373,10 @@
         return carry
 
     lax.fori_loop(0, BLOCKS, spread, 0, unroll=8)
-    reductions[1].middle()
 
     own_back = pltpu.make_async_copy(sg_ref.at[me], back_ref.at[:, columns(me)], sems["local"].at[5])
     own_back.start()
-
-    def send_back(k, carry):
-        to = shifted(at, (k * 37) % DEVICES)
-        remote(sg_ref.at[flat(to)], back_ref.at[:, columns(me)], sems["back_send"], sems["back_recv"], to, False)
-        return carry
-
-    lax.fori_loop(1, 64, send_back, 0)
+    to_all(0, 5, send_back)
 
     def terms0(i, carry):
         here = tile(i)
@@ -370,14 +385,17 @@
 
     lax.fori_loop(0, TILES, terms0, 0)
     reductions[0].send_tile(TILES - 1)
+    reductions[1].middle()
+    to_all(5, 7, send_back)
+    reductions[0].first()
     reductions[1].second()
-    reductions[0].first()
-    lax.fori_loop(64, 96, send_back, 0)
+    to_all(7, 10, send_back)
+    reductions[0].middle()
     reductions[1].third()
-    reductions[0].middle()
-    lax.fori_loop(96, DEVICES, send_back, 0)
+    to_all(10, 13, send_back)
+    reductions[0].second()
     reductions[1].last(sums_ref)
-    reductions[0].second()
+    to_all(13, 16, send_back)
     small = t_ref.at[pl.ds(0, DEVICES - 1)]
     pltpu.make_async_copy(small, small, sems["sum_recv"]).wait()
     total_ref[...] = jnp.sum(t_ref[...], axis=0)
@@ -418,6 +436,7 @@
             scratch += [VM((2, 4, n, 128), low), VM((2, 4, n, 128), low), VM((4, 4, n, 128), low),
                         VM((4, 4, n, 128), low), VM((3, 4, n, 128), low), VM((3, n, 128), low)]
     scratch += [pltpu.SemaphoreType.DMA(shape) if shape else pltpu.SemaphoreType.DMA for _, shape in SEMS]
+    scratch.append(pltpu.SemaphoreType.REGULAR((3,)))
     return pl.pallas_call(
         whole_kernel,
         out_shape=(jax.ShapeDtypeStruct((2, OWNED, 128), f32),
@@ -430,6 +449,54 @@
             has_side_effects=True, collective_id=0, vmem_limit_bytes=60 * 1024 * 1024),
         name="whole",
     )(slot_of_block, block_of_slot, pooled, dense, labels, weights, wide, mid, narrow, cross_in, cross_out, bias, head)
+
+
+PIECES = 4
+
+
+def post_kernel(back_ref, sums_ref, total_ref, pooled_ref, in_ref, out_ref, bias_ref):
+    scale = BATCH_ROWS / total_ref[...]
+    many = back_ref.shape[1] // 128
+    flat_rows = pooled_ref.reshape(BLOCK_WIDTH * many, 128)
+
+    def move(j, carry):
+        at = pl.ds(pl.multiple_of(j * 128, 128), 128)
+        flat_rows[pl.ds(j, BLOCK_WIDTH, stride=many), :] = back_ref[:, at].astype(jnp.float32) * scale
+        return carry
+
+    lax.fori_loop(0, many, move, 0, unroll=8)
+
+    @pl.when(pl.program_id(0) == 0)
+    def _():
+        for l in range(2):
+            for h in range(2):
+                rows = pl.ds(2 * h + l, SHARE, stride=4)
+                in_ref[rows, :] = sums_ref[l, pl.ds(h * SLOT, SHARE), :] * scale
+                out_ref[rows, :] = sums_ref[l, pl.ds((2 + h) * SLOT, SHARE), :] * scale
+            bias_ref[pl.ds(l, 1), :] = (sums_ref[l, pl.ds(SHARE, 1), :] * scale)[:, :SHARE]
+
+
+def post(returned, sums, total):
+    f32 = jnp.float32
+    many = DEVICES * ROWS // 128
+    once = lambda shape: pl.BlockSpec(shape, lambda i: (0,) * len(shape))
+    return pl.pallas_call(
+        post_kernel,
+        grid=(PIECES,),
+        out_shape=(jax.ShapeDtypeStruct((BLOCK_WIDTH, many, 128), f32),
+                   jax.ShapeDtypeStruct((4 * SHARE, 128), f32),
+                   jax.ShapeDtypeStruct((4 * SHARE, 128), f32),
+                   jax.ShapeDtypeStruct((2, SHARE), f32)),
+        in_specs=[pl.BlockSpec((BLOCK_WIDTH, DEVICES * ROWS // PIECES), lambda i: (0, i)),
+                  once((2, OWNED, 128)), once((1, 128))],
+        out_specs=(pl.BlockSpec((BLOCK_WIDTH, many // PIECES, 128), lambda i: (0, i, 0)),
+                   once((4 * SHARE, 128)), once((4 * SHARE, 128)), once((2, SHARE))),
+        name="post",
+    )(returned, sums, total)
+
+
+def unpacked(rows):
+    return jnp.transpose(rows.reshape(SHARE, 2, 2, 128), (2, 0, 1, 3)).reshape(2, SHARE, 256)
 
 
 def body(
@@ -446,13 +513,12 @@
     cross_bias,
     head_weight,
 ):
-    batch_rows = pooled.shape[2]
     numbers = jnp.arange(BLOCKS, dtype=jnp.int32)
-    block_of_slot = jnp.sum(jnp.where(slot_of_block[None, :] == numbers[:, None], numbers[None, :], 0), 1)
+    block_of_slot = jnp.max(jnp.where(slot_of_block[None, :] == numbers[:, None], numbers[None, :], 0), 1)
     sums, returned, total = whole(
         slot_of_block,
         block_of_slot,
-        pooled.reshape(BLOCK_WIDTH, batch_rows),
+        pooled.reshape(BLOCK_WIDTH, BATCH_ROWS),
         dense_part,
         labels[None],
         sample_weight[None],
@@ -462,14 +528,15 @@
         cross_in,
         cross_out,
         cross_bias,
-        head_weight[None],
+        head_weight,
     )
-    scale = batch_rows / total[0, 0]
-    sums = sums.reshape(2, 2, 2, SLOT, 128) * scale
-    whole_sums = jnp.moveaxis(sums[:, :, :, :SHARE], 2, 3).reshape(2, 2, SHARE, 256)
-    grad_bias = sums[:, 0, 0, SHARE, :SHARE]
-    pooled_grad = (returned.astype(jnp.float32) * scale).reshape(BLOCK_WIDTH, 1, batch_rows)
-    return (pooled_grad, whole_sums[:, 0], jnp.swapaxes(whole_sums[:, 1], 1, 2), grad_bias)
+    pooled_grad, grad_in, grad_out, grad_bias = post(returned, sums, total)
+    return (
+        pooled_grad.reshape(BLOCK_WIDTH, 1, BATCH_ROWS),
+        unpacked(grad_in),
+        jnp.swapaxes(unpacked(grad_out), 1, 2),
+        grad_bias,
+    )
 
 
 def solution(mesh):

time: 100 us -> 94 us (0.940)
  local copies, waits for them, and re-layouts: 6.24 us -> 2.95 us
  other arithmetic: 3.56 us -> 1.28 us
    pallas_call x1, Pallas kernels: 89 us -> 84.3 us  [whole(): pl.pallas_call(whole_kernel, out_shape=(jax.ShapeDtypeStruct((2, OWNED, 1...]
    pallas_call x0 -> x1, Pallas kernels: none -> 4.51 us  [post(): pl.pallas_call(post_kernel, grid=(PIECES,), out_shape=(jax.ShapeDtypeStru...]
    unnamed x1 -> x0, local copies, waits for them, and re-layouts: 3.48 us -> none
    reshape x1 -> x2, local copies, waits for them, and re-layouts: 0.13 us -> 2.95 us  [unpacked(): rows.reshape(SHARE, 2, 2, 128)]
    reshape x1 -> x0, other arithmetic: 1.36 us -> none  [body(): (returned.astype(jnp.float32) * scale).reshape(BLOCK_WIDTH, 1, batch_rows)]
    broadcast_in_dim x1 -> x0, local copies, waits for them, and re-layouts: 1.33 us -> none  [body(): head_weight[None]]
    reduce_max x0 -> x1, other arithmetic: none -> 1.28 us  [body(): jnp.max(jnp.where(slot_of_block[None, :] == numbers[:, None], numbers[Non...]
    reduce_sum x1 -> x0, other arithmetic: 1.28 us -> none  [body(): jnp.sum(jnp.where(slot_of_block[None, :] == numbers[:, None], numbers[Non...]
where the time goes in v3:
time: 94 us; the launch traced here: 93.7 us
  Pallas kernels  88.9 us (95%)
  local copies, waits for them, and re-layouts  2.95 us (3%)
  other arithmetic  1.28 us (1%)
    pallas_call x1, Pallas kernels, whole(): pl.pallas_call(whole_kernel, out_shape=(jax.ShapeDtypeStruct((2, OWNED, 1...  84.3 us
    pallas_call x1, Pallas kernels, post(): pl.pallas_call(post_kernel, grid=(PIECES,), out_shape=(jax.ShapeDtypeStru...  4.51 us
    reshape x2, local copies, waits for them, and re-layouts, unpacked(): rows.reshape(SHARE, 2, 2, 128)  2.95 us

profile of v3, /device:TPU:0, one launch (start us, length us, event | category | flops | bytes accessed | tf_op | source)
XLA Modules:
  0.0 93.7 jit_solution(6254401210461838714)
XLA Ops:
  0.6 1.3 %select_reduce_fusion.block_ref = s32[128]{0:T(128)} fusion(s32[128]{0:T(128)} %slot_ref.1), kind=kLoop, calls=%fused_computation | loop fusion | flops 49024 | bytes 1024 | tf_op jit(solution)/shard_map/reduce_max | solution.py:517
  1.9 84.3 %whole.1 = (f32[2,128,128]{2,1,0:T(8,128)}, bf16[16,32768]{1,0:T(8,128)(2,1)}, f32[1,128]{1,0:T(1,128)}) custom-call(s32[128]{0:T(128)} %slot_ref.1, s32[128]{0:T(128)} %select_reduce_fusion.block_ref, bf16[16,32768]{1,0:T(8,128)(2,1)} %bitcast.12, bf16[128,256]{1,0:T(8,128)(2,1)} %dense_ref.1, s32[1,256]{1,0:T(1,128)} %bitcast.15, f32[1,256]{1,0:T(1,128)} %bitcast.16, ...), custom_call_target="tpu_custom_call" | custom-call | tf_op jit(solution)/shard_map/whole/pallas_call | solution.py:440
  86.3 4.5 %post.1 = (f32[16,256,128]{2,1,0:T(8,128)}, f32[108,128]{1,0:T(8,128)}, f32[108,128]{1,0:T(8,128)}, f32[2,27]{1,0:T(2,128)}) custom-call(bf16[16,32768]{1,0:T(8,128)(2,1)} %get-tuple-element.11.back_ref, f32[2,128,128]{2,1,0:T(8,128)} %get-tuple-element.12.sums_ref, f32[1,128]{1,0:T(1,128)} %get-tuple-element.13.total_ref), custom_call_target="tpu_custom_call" | custom-call | tf_op jit(solution)/shard_map/post/pallas_call | solution.py:483
  90.8 1.5 %reshape.29 = f32[27,2,2,128]{3,2,1,0:T(2,128)} reshape(f32[108,128]{1,0:T(8,128)} %get-tuple-element.15) | data formatting | bytes 110592 | tf_op jit(solution)/shard_map/reshape | solution.py:499
  92.2 1.5 %reshape.31 = f32[27,2,2,128]{3,2,1,0:T(2,128)} reshape(f32[108,128]{1,0:T(8,128)} %get-tuple-element.16) | data formatting | bytes 110592 | tf_op jit(solution)/shard_map/reshape | solution.py:499

commit v4 on v3

--- a/solution.py
+++ b/solution.py
@@ -26,6 +26,25 @@
     ((0, 32, (0, 1, 2)), (32, 80, (1, 2, 0)), (80, 128, (2, 0, 1))),
     ((0, 48, (0, 1, 2)), (48, 96, (1, 2, 0)), (96, 128, (2, 0, 1))),
 )
+
+
+def known_after(x, z, y, c):
+    others = (x != 0) + (c != 0)
+    if others + (z != 0) + (y != 0) == 1:
+        return 0
+    if not z:
+        return 1 if y and others == 1 else 3
+    return 2 if others < 2 else 3
+
+
+def sends_of(rounds):
+    steps = [((k // 32), (k // 8) % 4, (k // 2) % 4, k % 2) for k in [(37 * i) % 128 for i in range(1, 128)]]
+    steps = [step for step in steps if (known_after(*step) if sum(map(bool, step)) != 2 or not (
+        step[1] and step[2]) else 1) == rounds]
+    return sorted(steps, key=lambda step: -sum(min(v, 4 - v) for v in step[:3]))
+
+
+FORWARD = [sends_of(rounds) for rounds in range(4)]
 TURN_X = (0, 1, 2, 3, 1, 2, 3, 0)
 TURN_Z = (0, 2, 1, 3, 3, 1, 0, 2)
 HALVES = (pl.ds(0, 2), pl.ds(2, 2))
@@ -211,11 +230,10 @@
     local_sum = jnp.sum(weight_ref[...], axis=1, keepdims=True)
     w_ref[...] = jnp.broadcast_to(local_sum, (1, 128))
     t_ref[me] = jnp.broadcast_to(local_sum, (1, 128))
-    pl.semaphore_wait(barrier, len(near))
-    for d in (2, 1, 0):
-        for device in lines[d]:
-            pl.semaphore_signal(sems["round"].at[d], inc=1, device_id=device, device_id_type=MESH)
-        pl.semaphore_wait(sems["round"].at[d], 3)
+    ys = [(at[2] + q) % 4 for q in range(4)]
+    cores = [at[3], 1 - at[3]]
+    xs_now = [(at[0] + q) % 4 for q in range(4)]
+    zs_now = [(at[1] + q) % 4 for q in range(4)]
 
     def to_all(lo, hi, send):
         def some(i, carry):
@@ -231,8 +249,6 @@
                     send(to)
             return carry
 
-        ys = [(at[2] + q) % 4 for q in range(4)]
-        cores = [at[3], 1 - at[3]]
         lax.fori_loop(lo, hi, some, 0)
 
     def send_forward(to):
@@ -244,7 +260,18 @@
     def send_back(to):
         remote(sg_ref.at[flat(to)], back_ref.at[:, columns(me)], sems["back_send"], sems["back_recv"], to, False)
 
-    to_all(0, 16, send_forward)
+    def to_known(rounds):
+        for x, z, y, c in FORWARD[rounds]:
+            send_forward((xs_now[x], zs_now[z], ys[y], cores[c]))
+
+    pl.semaphore_wait(barrier, len(near))
+    for d in (2, 1, 0):
+        for device in lines[d]:
+            pl.semaphore_signal(sems["round"].at[d], inc=1, device_id=device, device_id_type=MESH)
+        to_known(2 - d)
+        pl.semaphore_wait(sems["round"].at[d], 3)
+    to_known(3)
+
 
     row = lax.broadcasted_iota(jnp.int32, (TILE, 128), 0)
     lane = lax.broadcasted_iota(jnp.int32, (TILE, 128), 1)
@@ -293,7 +320,7 @@
         layer[here, :] = (s * gate + s).astype(low)
         return carry
 
-    lax.fori_loop(0, TILES, forward0, 0)
+    lax.fori_loop(0, TILES, forward0, 0, unroll=2)
     hidden1 = contract(in_t[1], layer[...], 1, 0).astype(low)
 
     def forward1(i, logit):
@@ -303,7 +330,7 @@
         last = (start[here, :].astype(f32) * gate + layer[here, :].astype(f32)).astype(low).astype(f32)
         return logit + jnp.sum((col[here, 2:3] * last).reshape(TILE // 8, 8, ROWS), axis=0)
 
-    logit = lax.fori_loop(0, TILES, forward1, jnp.zeros((8, ROWS), f32))
+    logit = lax.fori_loop(0, TILES, forward1, jnp.zeros((8, ROWS), f32), unroll=2)
     logit = jnp.sum(logit, axis=0, keepdims=True)
     signal = weight_ref[...] * (jax.nn.sigmoid(logit) - label_ref[...].astype(f32))
 
@@ -319,7 +346,7 @@
         low1[here, :] = gate_grad.astype(low)
         return carry
 
-    lax.fori_loop(0, TILES, backward1, 0)
+    lax.fori_loop(0, TILES, backward1, 0, unroll=2)
     grad1 = contract(out_ref[1], low1[...], 1, 0).astype(low)
     bias_row = lax.broadcasted_iota(jnp.int32, (SLOT, 128), 0) == SHARE
     reductions = [
@@ -352,7 +379,7 @@
         gate0[here, :] = gate1[here, :] * above + gate0[here, :] * upstream + upstream
         return carry
 
-    lax.fori_loop(0, TILES, backward0, 0)
+    lax.fori_loop(0, TILES, backward0, 0, unroll=2)
     reductions[1].send_tile(TILES - 1)
     grad0 = contract(out_ref[0], low0[...], 1, 0).astype(low)
     reductions[1].first()
@@ -362,7 +389,7 @@
         low1[here, :] = (gate0[here, :] + contract(in_ref[0, here, :], grad0, 1, 0)).astype(low)
         return carry
 
-    lax.fori_loop(0, TILES, finish, 0)
+    lax.fori_loop(0, TILES, finish, 0, unroll=2)
     for n, (which, t, column, width) in enumerate(table_rows()):
         lg_ref[pl.ds(column // 16, width // 16)] = contract(
             projections[which][t], low1[pl.ds(128 + n * 128, 128), :], 1, 0).astype(low).reshape(
@@ -383,7 +410,7 @@
         pack(0, i, contract(start[here, :], grad0, 1, 1), contract(low0[here, :], hidden0, 1, 1))
         return carry
 
-    lax.fori_loop(0, TILES, terms0, 0)
+    lax.fori_loop(0, TILES, terms0, 0, unroll=2)
     reductions[0].send_tile(TILES - 1)
     reductions[1].middle()
     to_all(5, 7, send_back)
@@ -451,28 +478,27 @@
     )(slot_of_block, block_of_slot, pooled, dense, labels, weights, wide, mid, narrow, cross_in, cross_out, bias, head)
 
 
-PIECES = 4
+PIECES = 2
 
 
 def post_kernel(back_ref, sums_ref, total_ref, pooled_ref, in_ref, out_ref, bias_ref):
     scale = BATCH_ROWS / total_ref[...]
     many = back_ref.shape[1] // 128
-    flat_rows = pooled_ref.reshape(BLOCK_WIDTH * many, 128)
 
     def move(j, carry):
-        at = pl.ds(pl.multiple_of(j * 128, 128), 128)
-        flat_rows[pl.ds(j, BLOCK_WIDTH, stride=many), :] = back_ref[:, at].astype(jnp.float32) * scale
-        return carry
-
-    lax.fori_loop(0, many, move, 0, unroll=8)
+        part = back_ref[:, pl.ds(pl.multiple_of(j * 1024, 1024), 1024)].astype(jnp.float32) * wide
+        pooled_ref[:, pl.ds(pl.multiple_of(j * 8, 8), 8), :] = pltpu.einshape("c(jl)->cjl", part, j=8, l=128)
+        return carry
+
+    wide = jnp.tile(scale, (1, 8))
+    lax.fori_loop(0, many // 8, move, 0, unroll=2)
 
     @pl.when(pl.program_id(0) == 0)
     def _():
         for l in range(2):
             for h in range(2):
-                rows = pl.ds(2 * h + l, SHARE, stride=4)
-                in_ref[rows, :] = sums_ref[l, pl.ds(h * SLOT, SHARE), :] * scale
-                out_ref[rows, :] = sums_ref[l, pl.ds((2 + h) * SLOT, SHARE), :] * scale
+                in_ref[:, h, l, :] = sums_ref[l, pl.ds(h * SLOT, SHARE), :] * scale
+                out_ref[:, h, l, :] = sums_ref[l, pl.ds((2 + h) * SLOT, SHARE), :] * scale
             bias_ref[pl.ds(l, 1), :] = (sums_ref[l, pl.ds(SHARE, 1), :] * scale)[:, :SHARE]
 
 
@@ -484,19 +510,19 @@
         post_kernel,
         grid=(PIECES,),
         out_shape=(jax.ShapeDtypeStruct((BLOCK_WIDTH, many, 128), f32),
-                   jax.ShapeDtypeStruct((4 * SHARE, 128), f32),
-                   jax.ShapeDtypeStruct((4 * SHARE, 128), f32),
+                   jax.ShapeDtypeStruct((SHARE, 2, 2, 128), f32),
+                   jax.ShapeDtypeStruct((SHARE, 2, 2, 128), f32),
                    jax.ShapeDtypeStruct((2, SHARE), f32)),
         in_specs=[pl.BlockSpec((BLOCK_WIDTH, DEVICES * ROWS // PIECES), lambda i: (0, i)),
                   once((2, OWNED, 128)), once((1, 128))],
         out_specs=(pl.BlockSpec((BLOCK_WIDTH, many // PIECES, 128), lambda i: (0, i, 0)),
-                   once((4 * SHARE, 128)), once((4 * SHARE, 128)), once((2, SHARE))),
+                   once((SHARE, 2, 2, 128)), once((SHARE, 2, 2, 128)), once((2, SHARE))),
         name="post",
     )(returned, sums, total)
 
 
 def unpacked(rows):
-    return jnp.transpose(rows.reshape(SHARE, 2, 2, 128), (2, 0, 1, 3)).reshape(2, SHARE, 256)
+    return jnp.transpose(rows, (2, 0, 1, 3)).reshape(2, SHARE, 256)
 
 
 def body(

time: 94 us -> 83 us (0.88)
  Pallas kernels: 88.9 us -> 81 us
  local copies, waits for them, and re-layouts: 2.95 us -> 0 us
    pallas_call x1, Pallas kernels: 84.3 us -> 78.2 us  [whole(): pl.pallas_call(whole_kernel, out_shape=(jax.ShapeDtypeStruct((2, OWNED, 1...]
    reshape x2 -> x0, local copies, waits for them, and re-layouts: 2.95 us -> none  [unpacked(): rows.reshape(SHARE, 2, 2, 128)]
    pallas_call x1, Pallas kernels: 4.51 us -> 2.78 us  [post(): pl.pallas_call(post_kernel, grid=(PIECES,), out_shape=(jax.ShapeDtypeStru...]
where the time goes in v4:
time: 83 us; the launch traced here: 82.9 us
  Pallas kernels  81 us (98%)
  other arithmetic  1.28 us (2%)
    pallas_call x1, Pallas kernels, whole(): pl.pallas_call(whole_kernel, out_shape=(jax.ShapeDtypeStruct((2, OWNED, 1...  78.2 us
    pallas_call x1, Pallas kernels, post(): pl.pallas_call(post_kernel, grid=(PIECES,), out_shape=(jax.ShapeDtypeStru...  2.78 us

profile of v4, /device:TPU:0, one launch (start us, length us, event | category | flops | bytes accessed | tf_op | source)
XLA Modules:
  0.0 82.9 jit_solution(3511767158652301583)
XLA Ops:
  0.6 1.3 %select_reduce_fusion.block_ref = s32[128]{0:T(128)} fusion(s32[128]{0:T(128)} %slot_ref.1), kind=kLoop, calls=%fused_computation | loop fusion | flops 49024 | bytes 1024 | tf_op jit(solution)/shard_map/reduce_max | solution.py:543
  1.9 78.2 %whole.1 = (f32[2,128,128]{2,1,0:T(8,128)}, bf16[16,32768]{1,0:T(8,128)(2,1)}, f32[1,128]{1,0:T(1,128)}) custom-call(s32[128]{0:T(128)} %slot_ref.1, s32[128]{0:T(128)} %select_reduce_fusion.block_ref, bf16[16,32768]{1,0:T(8,128)(2,1)} %bitcast.12, bf16[128,256]{1,0:T(8,128)(2,1)} %dense_ref.1, s32[1,256]{1,0:T(1,128)} %bitcast.13, f32[1,256]{1,0:T(1,128)} %bitcast.14, ...), custom_call_target="tpu_custom_call" | custom-call | tf_op jit(solution)/shard_map/whole/pallas_call | solution.py:467
  80.1 2.8 %post.1 = (f32[16,256,128]{2,1,0:T(8,128)}, f32[27,2,2,128]{3,2,1,0:T(2,128)}, f32[27,2,2,128]{3,2,1,0:T(2,128)}, f32[2,27]{1,0:T(2,128)}) custom-call(bf16[16,32768]{1,0:T(8,128)(2,1)} %get-tuple-element.11.back_ref, f32[2,128,128]{2,1,0:T(8,128)} %get-tuple-element.12.sums_ref, f32[1,128]{1,0:T(1,128)} %get-tuple-element.13.total_ref), custom_call_target="tpu_custom_call" | custom-call | tf_op jit(solution)/shard_map/post/pallas_call | solution.py:509

commit v5 on v4

--- a/solution.py
+++ b/solution.py
@@ -21,9 +21,10 @@
 SHARE = 27
 SLOT = 32
 OWNED = 128
+CLOSE = 112
 VM = pltpu.VMEM
 PARTS = (
-    ((0, 32, (0, 1, 2)), (32, 80, (1, 2, 0)), (80, 128, (2, 0, 1))),
+    ((0, 32, (0, 1, 2)), (32, 64, (1, 2, 0)), (64, 112, (2, 0, 1))),
     ((0, 48, (0, 1, 2)), (48, 96, (1, 2, 0)), (96, 128, (2, 0, 1))),
 )
 
@@ -186,13 +187,13 @@
 SEMS = (("core_send", (2,)), ("core_recv", (2,)), ("one_send", (2, 3, 6)), ("one_recv", (2, 3, 6)),
         ("two_send", (2, 3, 3)), ("two_recv", (2, 3, 3)), ("three_send", (2, 3, 3)), ("three_recv", (2, 3, 3)),
         ("fwd_send", ()), ("fwd_recv", ()), ("sum_send", ()), ("sum_recv", ()), ("back_send", ()),
-        ("back_recv", ()), ("local", (7,)))
-
-
-def whole_kernel(slot_ref, block_ref, x_ref, dense_ref, label_ref, weight_ref, wide_ref, mid_ref, narrow_ref,
-                 in_hbm, out_hbm, bias_in, head_ref, sums_ref, back_ref, total_ref,
-                 slots_ref, w_ref, t_ref, in_ref, out_ref, in_t, out_t, vec_ref, col, cols_ref, sg_ref, lg_ref, start, layer,
-                 low0, low1, gate0, gate1, stage, bias_ref, owner_mask, place_mask, *rest):
+        ("back_recv", ()), ("local", (13,)))
+
+
+def whole_kernel(slot_ref, block_ref, x_ref, dense_hbm, label_ref, weight_ref, wide_hbm, mid_hbm, narrow_hbm,
+                 in_hbm, out_hbm, bias_hbm, head_hbm, sums_ref, back_ref, total_ref,
+                 dense_ref, wide_ref, mid_ref, narrow_ref, bias_in, head_ref, slots_ref, w_ref, t_ref, in_ref, out_ref, in_t, out_t, vec_ref, col, cols_ref, sg_ref, lg_ref, start, layer,
+                 low0, low1, gate0, gate1, stage, bias_ref, owner_mask, place_mask, close, *rest):
     low = jnp.bfloat16
     f32 = jnp.float32
     projections = (wide_ref, mid_ref, narrow_ref)
@@ -223,7 +224,11 @@
     for l in range(2):
         loads.append(pltpu.make_async_copy(in_hbm.at[l], in_ref.at[l], sems["local"].at[l]))
         loads.append(pltpu.make_async_copy(out_hbm.at[l], out_ref.at[l], sems["local"].at[2 + l]))
-    for load in loads:
+    small_loads = [
+        pltpu.make_async_copy(src, dst, sems["local"].at[7 + n]) for n, (src, dst) in enumerate((
+            (dense_hbm, dense_ref), (wide_hbm, wide_ref), (mid_hbm, mid_ref), (narrow_hbm, narrow_ref),
+            (bias_hbm, bias_in), (head_hbm, head_ref)))]
+    for load in small_loads + loads:
         load.start()
     own = pltpu.make_async_copy(x_ref.at[:, columns(me)], slots_ref.at[me], sems["local"].at[4])
     own.start()
@@ -281,6 +286,8 @@
     owner_mask[...] = jnp.where(owner_lane // SHARE == owner_row, 1.0, 0.0).astype(low)
     for g in range(4):
         stage[g, pl.ds(TILE, 8), :] = jnp.zeros((8, 128), f32)
+    for load in small_loads:
+        load.wait()
     vec_ref[...] = jnp.zeros(vec_ref.shape, f32)
     vec_ref[pl.ds(0, 2), :] = bias_in[...]
     for i in range(WIDTH // 128):
@@ -320,7 +327,7 @@
         layer[here, :] = (s * gate + s).astype(low)
         return carry
 
-    lax.fori_loop(0, TILES, forward0, 0, unroll=2)
+    lax.fori_loop(0, TILES, forward0, 0, unroll=4)
     hidden1 = contract(in_t[1], layer[...], 1, 0).astype(low)
 
     def forward1(i, logit):
@@ -330,7 +337,7 @@
         last = (start[here, :].astype(f32) * gate + layer[here, :].astype(f32)).astype(low).astype(f32)
         return logit + jnp.sum((col[here, 2:3] * last).reshape(TILE // 8, 8, ROWS), axis=0)
 
-    logit = lax.fori_loop(0, TILES, forward1, jnp.zeros((8, ROWS), f32), unroll=2)
+    logit = lax.fori_loop(0, TILES, forward1, jnp.zeros((8, ROWS), f32), unroll=4)
     logit = jnp.sum(logit, axis=0, keepdims=True)
     signal = weight_ref[...] * (jax.nn.sigmoid(logit) - label_ref[...].astype(f32))
 
@@ -346,7 +353,7 @@
         low1[here, :] = gate_grad.astype(low)
         return carry
 
-    lax.fori_loop(0, TILES, backward1, 0, unroll=2)
+    lax.fori_loop(0, TILES, backward1, 0, unroll=4)
     grad1 = contract(out_ref[1], low1[...], 1, 0).astype(low)
     bias_row = lax.broadcasted_iota(jnp.int32, (SLOT, 128), 0) == SHARE
     reductions = [
@@ -357,20 +364,35 @@
             stage[h, pl.ds(0, TILE), :] = in_term[:, h * 128:(h + 1) * 128]
             stage[2 + h, pl.ds(0, TILE), :] = out_term[:, h * 128:(h + 1) * 128]
         for o in range(OWNERS):
+            block = (i // 2, 2 * (i % 2) + o // 8, (o // 2) % 4, o % 2)
+            if l == 0:
+                for g in range(4):
+                    close[o % 4, pl.ds(SHARE * g, SLOT), :] = stage[g, pl.ds(SHARE * o, SLOT), :]
+                close[o % 4, pl.ds(4 * SHARE, 1), :] = bias_ref[l, pl.ds(i * OWNERS + o, 1), :]
+                grads[l][block] = close[o % 4, pl.ds(0, CLOSE), :].astype(low)
+                continue
             for g in range(4):
                 piece = stage[g, pl.ds(SHARE * o, SLOT), :]
                 if g == 0:
                     piece = jnp.where(bias_row, bias_ref[l, pl.ds(i * OWNERS + o, 1), :], piece)
-                grads[l][i // 2, 2 * (i % 2) + o // 8, (o // 2) % 4, o % 2, pl.ds(g * SLOT, SLOT), :] = (
+                grads[l][block + (pl.ds(g * SLOT, SLOT), slice(None))] = (
                     piece.astype(low))
 
         @pl.when(i > 0)
         def _():
             reductions[l].send_tile(i - 1)
 
+    def terms1(i, carry):
+        here = tile(i)
+        pack(1, i, contract(layer[here, :], grad1, 1, 1), contract(low1[here, :], hidden1, 1, 1))
+        return carry
+
+    lax.fori_loop(0, TILES, terms1, 0, unroll=2)
+    reductions[1].send_tile(TILES - 1)
+    reductions[1].first()
+
     def backward0(i, carry):
         here = tile(i)
-        pack(1, i, contract(layer[here, :], grad1, 1, 1), contract(low1[here, :], hidden1, 1, 1))
         above = col[here, 2:3] * signal
         upstream = above + contract(in_ref[1, here, :], grad1, 1, 0)
         gate_grad = start[here, :].astype(f32) * upstream
@@ -380,16 +402,15 @@
         return carry
 
     lax.fori_loop(0, TILES, backward0, 0, unroll=2)
-    reductions[1].send_tile(TILES - 1)
     grad0 = contract(out_ref[0], low0[...], 1, 0).astype(low)
-    reductions[1].first()
+    reductions[1].middle()
 
     def finish(i, carry):
         here = tile(i)
         low1[here, :] = (gate0[here, :] + contract(in_ref[0, here, :], grad0, 1, 0)).astype(low)
         return carry
 
-    lax.fori_loop(0, TILES, finish, 0, unroll=2)
+    lax.fori_loop(0, TILES, finish, 0, unroll=4)
     for n, (which, t, column, width) in enumerate(table_rows()):
         lg_ref[pl.ds(column // 16, width // 16)] = contract(
             projections[which][t], low1[pl.ds(128 + n * 128, 128), :], 1, 0).astype(low).reshape(
@@ -403,25 +424,23 @@
 
     own_back = pltpu.make_async_copy(sg_ref.at[me], back_ref.at[:, columns(me)], sems["local"].at[5])
     own_back.start()
-    to_all(0, 5, send_back)
-
     def terms0(i, carry):
         here = tile(i)
         pack(0, i, contract(start[here, :], grad0, 1, 1), contract(low0[here, :], hidden0, 1, 1))
         return carry
 
+    to_all(0, 5, send_back)
     lax.fori_loop(0, TILES, terms0, 0, unroll=2)
     reductions[0].send_tile(TILES - 1)
-    reductions[1].middle()
+    reductions[1].second()
     to_all(5, 7, send_back)
     reductions[0].first()
-    reductions[1].second()
+    reductions[1].third()
     to_all(7, 10, send_back)
     reductions[0].middle()
-    reductions[1].third()
+    reductions[1].last(sums_ref)
     to_all(10, 13, send_back)
     reductions[0].second()
-    reductions[1].last(sums_ref)
     to_all(13, 16, send_back)
     small = t_ref.at[pl.ds(0, DEVICES - 1)]
     pltpu.make_async_copy(small, small, sems["sum_recv"]).wait()
@@ -449,14 +468,18 @@
     activation = VM((WIDTH, ROWS), low)
     full = VM((WIDTH, ROWS), f32)
     scratch = [
+        VM((128, ROWS), low), VM(wide.shape, low), VM(mid.shape, low), VM(narrow.shape, low), VM(bias.shape, f32),
+        VM(head.shape, f32),
         VM((DEVICES, 16, ROWS), low), VM((1, 128), f32), VM((DEVICES, 1, 128), f32),
         VM((2, WIDTH, 256), low), VM((2, 256, WIDTH), low), VM((2, 256, WIDTH), low), VM((2, WIDTH, 256), low),
         VM((8, WIDTH), f32), VM((WIDTH, 8), f32), VM((2048, ROWS), low), VM((DEVICES, 16, ROWS), low),
         VM((DEVICES, 16, ROWS), low),
         activation, activation, activation, activation, full, full,
         VM((4, TILE + 8, 128), f32), VM((2, DEVICES, 128), f32), VM((OWNERS, TILE), low), VM((TILE, 128), f32),
+        VM((4, 120, 128), f32),
     ]
-    scratch += [VM((4, 4, 4, 2, OWNED, 128), low)] * 2 + [VM((4, 4, 4, OWNED, 128), low)] * 2
+    scratch += [VM((4, 4, 4, 2, n, 128), low) for n in (CLOSE, OWNED)]
+    scratch += [VM((4, 4, 4, n, 128), low) for n in (CLOSE, OWNED)]
     for l in range(2):
         for lo, hi, _ in PARTS[l]:
             n = hi - lo
@@ -469,7 +492,7 @@
         out_shape=(jax.ShapeDtypeStruct((2, OWNED, 128), f32),
                    jax.ShapeDtypeStruct((16, DEVICES * ROWS), low),
                    jax.ShapeDtypeStruct((1, 128), f32)),
-        in_specs=[smem, smem, hbm] + [vmem] * 6 + [hbm, hbm, vmem, vmem],
+        in_specs=[smem, smem, hbm, hbm, vmem, vmem] + [hbm] * 7,
         out_specs=(vmem, vmem, vmem),
         scratch_shapes=scratch,
         compiler_params=pltpu.CompilerParams(
@@ -497,9 +520,10 @@
     def _():
         for l in range(2):
             for h in range(2):
-                in_ref[:, h, l, :] = sums_ref[l, pl.ds(h * SLOT, SHARE), :] * scale
-                out_ref[:, h, l, :] = sums_ref[l, pl.ds((2 + h) * SLOT, SHARE), :] * scale
-            bias_ref[pl.ds(l, 1), :] = (sums_ref[l, pl.ds(SHARE, 1), :] * scale)[:, :SHARE]
+                step = (SHARE, SLOT)[l]
+                in_ref[:, h, l, :] = sums_ref[l, pl.ds(h * step, SHARE), :] * scale
+                out_ref[:, h, l, :] = sums_ref[l, pl.ds((2 + h) * step, SHARE), :] * scale
+            bias_ref[pl.ds(l, 1), :] = (sums_ref[l, pl.ds((4 * SHARE, SHARE)[l], 1), :] * scale)[:, :SHARE]
 
 
 def post(returned, sums, total):

time: 83 us -> 79.2 us (0.954)
  Pallas kernels: 81 us -> 77.1 us
    pallas_call x1, Pallas kernels: 78.2 us -> 74.3 us  [whole(): pl.pallas_call(whole_kernel, out_shape=(jax.ShapeDtypeStruct((2, OWNED, 1...]
where the time goes in v5:
time: 79.2 us; the launch traced here: 79 us
  Pallas kernels  77.1 us (97%)
  other arithmetic  1.28 us (2%)
    pallas_call x1, Pallas kernels, whole(): pl.pallas_call(whole_kernel, out_shape=(jax.ShapeDtypeStruct((2, OWNED, 1...  74.3 us
    pallas_call x1, Pallas kernels, post(): pl.pallas_call(post_kernel, grid=(PIECES,), out_shape=(jax.ShapeDtypeStru...  2.78 us

profile of v5, /device:TPU:0, one launch (start us, length us, event | category | flops | bytes accessed | tf_op | source)
XLA Modules:
  0.0 79.0 jit_solution(11437939372797380927)
XLA Ops:
  0.6 1.3 %select_reduce_fusion.block_ref = s32[128]{0:T(128)} fusion(s32[128]{0:T(128)} %slot_ref.1), kind=kLoop, calls=%fused_computation | loop fusion | flops 49024 | bytes 1024 | tf_op jit(solution)/shard_map/reduce_max | solution.py:567
  1.9 74.3 %whole.1 = (f32[2,128,128]{2,1,0:T(8,128)}, bf16[16,32768]{1,0:T(8,128)(2,1)}, f32[1,128]{1,0:T(1,128)}) custom-call(s32[128]{0:T(128)} %slot_ref.1, s32[128]{0:T(128)} %select_reduce_fusion.block_ref, bf16[16,32768]{1,0:T(8,128)(2,1)} %bitcast.12, bf16[128,256]{1,0:T(8,128)(2,1)} %dense_hbm.1, s32[1,256]{1,0:T(1,128)} %bitcast.13, f32[1,256]{1,0:T(1,128)} %bitcast.14, ...), custom_call_target="tpu_custom_call" | custom-call | tf_op jit(solution)/shard_map/whole/pallas_call | solution.py:490
  76.2 2.8 %post.1 = (f32[16,256,128]{2,1,0:T(8,128)}, f32[27,2,2,128]{3,2,1,0:T(2,128)}, f32[27,2,2,128]{3,2,1,0:T(2,128)}, f32[2,27]{1,0:T(2,128)}) custom-call(bf16[16,32768]{1,0:T(8,128)(2,1)} %get-tuple-element.11.back_ref, f32[2,128,128]{2,1,0:T(8,128)} %get-tuple-element.12.sums_ref, f32[1,128]{1,0:T(1,128)} %get-tuple-element.13.total_ref), custom_call_target="tpu_custom_call" | custom-call | tf_op jit(solution)/shard_map/post/pallas_call | solution.py:533

commit v6 on v5

--- a/solution.py
+++ b/solution.py
@@ -337,7 +337,7 @@
         last = (start[here, :].astype(f32) * gate + layer[here, :].astype(f32)).astype(low).astype(f32)
         return logit + jnp.sum((col[here, 2:3] * last).reshape(TILE // 8, 8, ROWS), axis=0)
 
-    logit = lax.fori_loop(0, TILES, forward1, jnp.zeros((8, ROWS), f32), unroll=4)
+    logit = lax.fori_loop(0, TILES, forward1, jnp.zeros((8, ROWS), f32), unroll=8)
     logit = jnp.sum(logit, axis=0, keepdims=True)
     signal = weight_ref[...] * (jax.nn.sigmoid(logit) - label_ref[...].astype(f32))
 
@@ -353,7 +353,7 @@
         low1[here, :] = gate_grad.astype(low)
         return carry
 
-    lax.fori_loop(0, TILES, backward1, 0, unroll=4)
+    lax.fori_loop(0, TILES, backward1, 0, unroll=8)
     grad1 = contract(out_ref[1], low1[...], 1, 0).astype(low)
     bias_row = lax.broadcasted_iota(jnp.int32, (SLOT, 128), 0) == SHARE
     reductions = [
@@ -387,7 +387,7 @@
         pack(1, i, contract(layer[here, :], grad1, 1, 1), contract(low1[here, :], hidden1, 1, 1))
         return carry
 
-    lax.fori_loop(0, TILES, terms1, 0, unroll=2)
+    lax.fori_loop(0, TILES, terms1, 0, unroll=4)
     reductions[1].send_tile(TILES - 1)
     reductions[1].first()
 
@@ -401,7 +401,7 @@
         gate0[here, :] = gate1[here, :] * above + gate0[here, :] * upstream + upstream
         return carry
 
-    lax.fori_loop(0, TILES, backward0, 0, unroll=2)
+    lax.fori_loop(0, TILES, backward0, 0, unroll=4)
     grad0 = contract(out_ref[0], low0[...], 1, 0).astype(low)
     reductions[1].middle()
 
@@ -430,7 +430,7 @@
         return carry
 
     to_all(0, 5, send_back)
-    lax.fori_loop(0, TILES, terms0, 0, unroll=2)
+    lax.fori_loop(0, TILES, terms0, 0, unroll=4)
     reductions[0].send_tile(TILES - 1)
     reductions[1].second()
     to_all(5, 7, send_back)

time: 79.2 us -> 77.8 us (0.982); the launches traced: 79 us -> 76.5 us
  Pallas kernels: 77.1 us -> 74.6 us
    pallas_call x1, Pallas kernels: 74.3 us -> 71.8 us  [whole(): pl.pallas_call(whole_kernel, out_shape=(jax.ShapeDtypeStruct((2, OWNED, 1...]
where the time goes in v6:
time: 77.8 us; the launch traced here: 76.5 us
  Pallas kernels  74.6 us (96%)
  other arithmetic  1.28 us (2%)
    pallas_call x1, Pallas kernels, whole(): pl.pallas_call(whole_kernel, out_shape=(jax.ShapeDtypeStruct((2, OWNED, 1...  71.8 us
    pallas_call x1, Pallas kernels, post(): pl.pallas_call(post_kernel, grid=(PIECES,), out_shape=(jax.ShapeDtypeStru...  2.78 us

profile of v6, /device:TPU:0, one launch (start us, length us, event | category | flops | bytes accessed | tf_op | source)
XLA Modules:
  0.0 76.5 jit_solution(17554351916602310089)
XLA Ops:
  0.6 1.3 %select_reduce_fusion.block_ref = s32[128]{0:T(128)} fusion(s32[128]{0:T(128)} %slot_ref.1), kind=kLoop, calls=%fused_computation | loop fusion | flops 49024 | bytes 1024 | tf_op jit(solution)/shard_map/reduce_max | solution.py:567
  1.9 71.8 %whole.1 = (f32[2,128,128]{2,1,0:T(8,128)}, bf16[16,32768]{1,0:T(8,128)(2,1)}, f32[1,128]{1,0:T(1,128)}) custom-call(s32[128]{0:T(128)} %slot_ref.1, s32[128]{0:T(128)} %select_reduce_fusion.block_ref, bf16[16,32768]{1,0:T(8,128)(2,1)} %bitcast.12, bf16[128,256]{1,0:T(8,128)(2,1)} %dense_hbm.1, s32[1,256]{1,0:T(1,128)} %bitcast.13, f32[1,256]{1,0:T(1,128)} %bitcast.14, ...), custom_call_target="tpu_custom_call" | custom-call | tf_op jit(solution)/shard_map/whole/pallas_call | solution.py:490
  73.7 2.8 %post.1 = (f32[16,256,128]{2,1,0:T(8,128)}, f32[27,2,2,128]{3,2,1,0:T(2,128)}, f32[27,2,2,128]{3,2,1,0:T(2,128)}, f32[2,27]{1,0:T(2,128)}) custom-call(bf16[16,32768]{1,0:T(8,128)(2,1)} %get-tuple-element.11.back_ref, f32[2,128,128]{2,1,0:T(8,128)} %get-tuple-element.12.sums_ref, f32[1,128]{1,0:T(1,128)} %get-tuple-element.13.total_ref), custom_call_target="tpu_custom_call" | custom-call | tf_op jit(solution)/shard_map/post/pallas_call | solution.py:533
